TPU v7x, 512 devices: a whole 4x4x16 slice. The times are simulated.
512 devices in a mesh: dp: 8 (over y, x_hi), row: 16 (over z), col: 4 (over x_lo, core).
Axes of the slice: x: 4 (x_hi: 2, x_lo: 2; x = x_hi * 2 + x_lo), y: 4, z: 16, core: 2. Of those that a mesh axis runs over, the one named last changes fastest.
Arguments:
- gate_pre: bfloat16 [4096, 14336], P(('dp', 'col'), 'row'), may hold values from -6 to 6
- up_pre: bfloat16 [4096, 14336], P(('dp', 'col'), 'row'), may hold values from -6 to 6
- out_grad: bfloat16 [4096, 4096], P(('dp', 'row'), 'col'), may hold values from -6 to 6
- down_weight: bfloat16 [14336, 4096], P('row', 'col'), may hold values from -0.046875 to 0.046875
Outputs:
- layer_out: bfloat16 [4096, 4096], P(('dp', 'row'), 'col')
- gate_grad: bfloat16 [4096, 14336], P(('dp', 'col'), 'row')
- up_grad: bfloat16 [4096, 14336], P(('dp', 'col'), 'row')
- weight_grad: float32 [14336, 4096], P(('row', 'dp'), 'col')
All inputs are finite; a program needn't handle non-finite values.
Results may differ from a plain program's by a relative error of at most 0.017.
Values may be sent and summed in bfloat16 or wider, within the bound.
No kernel may reach another device: no remote copies, remote signals or barrier semaphores. Data moves between devices by JAX's collectives and lax.ppermute only.
A program may use at most 64 MiB of HBM per device.

v0:
```python
import jax
import jax.numpy as jnp
from jax import lax
from jax.sharding import PartitionSpec as P

hold = lax.optimization_barrier


def shifted(array, axis, by):
    count = lax.axis_size(axis)
    return lax.ppermute(array, axis, [(i, (i + by) % count) for i in range(count)])


def pick(array, index):
    return lax.dynamic_index_in_dim(array, index, 0, keepdims=False)


def gather_apart(block):
    groups = [[k, k + 4, k + 8, k + 12] for k in range(4)]
    return lax.all_gather(block, "row", axis=0, tiled=False, axis_index_groups=groups)


def gather_near(same):
    low = lax.axis_index("row") & 3
    whole = jnp.zeros((4,) + same.shape, same.dtype)
    for by in (1, 15, 2, 0):
        got = same if by == 0 else shifted(same, "row", by)
        whole = lax.dynamic_update_slice(whole, got[:, None], (0, (low - by) & 3, 0, 0))
    return whole.reshape(-1, same.shape[-1])


def sum_over_row(parts):
    count = lax.axis_size("row")
    parts = parts.reshape((count, parts.shape[0] // count) + parts.shape[1:])
    parts = lax.all_to_all(parts, "row", 0, 0, tiled=True)
    return jnp.sum(parts.astype(jnp.float32), axis=0)


def sum_over_dp(parts):
    parts = parts.reshape((8, parts.shape[0] // 8) + parts.shape[1:])
    me = lax.axis_index("dp")
    y, x = me >> 1, me & 1
    total = pick(parts, me).astype(jnp.float32)
    for dy, dx in ((1, 0), (3, 0), (0, 1), (1, 1), (3, 1), (2, 0), (2, 1)):
        route = [(a * 2 + b, (a + dy) % 4 * 2 + (b + dx) % 2) for a in range(4) for b in range(2)]
        mine = pick(parts, ((y + dy) & 3) * 2 + ((x + dx) & 1))
        total = total + lax.ppermute(mine, "dp", route).astype(jnp.float32)
    return total


def sum_over_col(parts):
    parts = parts.reshape((2, 2, parts.shape[0] // 4) + parts.shape[1:])
    me = lax.axis_index("col")
    x, core = me >> 1, me & 1
    other = lax.dynamic_index_in_dim(parts, 1 - core, 1, keepdims=False)
    mine = lax.dynamic_index_in_dim(parts, core, 1, keepdims=False)
    other = lax.ppermute(other, "col", [(i, i ^ 1) for i in range(4)])
    pair = mine.astype(jnp.float32) + other.astype(jnp.float32)
    away = lax.ppermute(pick(pair, 1 - x).astype(jnp.bfloat16), "col", [(i, i ^ 2) for i in range(4)])
    return pick(pair, x) + away.astype(jnp.float32)


def shards(gate_pre, up_pre, out_grad, down_weight):
    grad_apart = gather_apart(out_grad)

    gate32 = gate_pre.astype(jnp.float32)
    up32 = up_pre.astype(jnp.float32)
    sgate = jax.nn.sigmoid(gate32)
    act = gate32 * sgate
    hidden, grad_apart = hold(((act * up32).astype(jnp.bfloat16), grad_apart))
    grad_all = gather_near(grad_apart)
    hidden_all = lax.all_gather(hidden, "col", axis=0, tiled=True)
    layer_parts = jnp.dot(hidden_all, down_weight, preferred_element_type=jnp.float32).astype(jnp.bfloat16)
    layer_out = sum_over_row(layer_parts).astype(jnp.bfloat16)

    hidden_all, grad_all = hold((hidden_all, grad_all))
    factor = 1.0 / (hidden_all.shape[0] * lax.axis_size("dp")) ** 0.5
    local_grad = (
        lax.dot_general(
            hidden_all, grad_all, (((0,), (0,)), ((), ())), preferred_element_type=jnp.float32
        )
        * factor
    ).astype(jnp.bfloat16)
    local_grad, grad_late = hold((local_grad, grad_all))
    weight_grad = sum_over_dp(local_grad)
    dhidden = sum_over_col(
        lax.dot_general(
            grad_late, down_weight, (((1,), (1,)), ((), ())), preferred_element_type=jnp.float32
        ).astype(jnp.bfloat16)
    )
    up_grad = (dhidden * act).astype(jnp.bfloat16)
    gate_grad = (dhidden * up32 * sgate * (1.0 + gate32 * (1.0 - sgate))).astype(jnp.bfloat16)
    return (layer_out, gate_grad, up_grad, weight_grad)


def solution(mesh):
    return jax.shard_map(
        shards,
        mesh=mesh,
        in_specs=(
            P(("dp", "col"), "row"),
            P(("dp", "col"), "row"),
            P(("dp", "row"), "col"),
            P("row", "col"),
        ),
        out_specs=(
            P(("dp", "row"), "col"),
            P(("dp", "col"), "row"),
            P(("dp", "col"), "row"),
            P(("row", "dp"), "col"),
        ),
        check_vma=False,
    )
```

profile of v0, /device:TPU:32, one launch (start us, length us, event | category | flops | bytes accessed | tf_op | source)
XLA Modules:
  0.0 162.4 jit_solution(3433628262614967642)
XLA Ops:
  0.6 26.3 %all-gather = bf16[128,1024]{1,0:T(8,128)(2,1)S(1)} all-gather(bf16[32,1024]{1,0:T(8,128)(2,1)} %param.6), channel_id=2, replica_groups={{0,16,32,48},{4,20,36,52},{8,24,40,56},{12,28,44,60},{1,17,33,49},{5,21..., dimensions={0}, use_global_device_ids=true | all-gather | bytes 327680 | tf_op jit(solution)/shard_map/all_gather | solution.py:20
  28.2 9.3 %all_gather.11 = bf16[512,896]{1,0:T(8,128)(2,1)S(1)} all-gather(bf16[128,896]{1,0:T(8,128)(2,1)S(1)} %fusion), channel_id=1, replica_groups=mesh['dp'=8,'row'=16,'col'=4] {'col'}, dimensions={0}, use_global_device_ids=true | all-gather | bytes 1146880 | tf_op jit(solution)/shard_map/all_gather | solution.py:72
  37.5 2.3 %convolution_convert_fusion = bf16[512,1024]{1,0:T(8,128)(2,1)} fusion(bf16[512,896]{1,0:T(8,128)(2,1)S(1)} %all_gather.11, bf16[896,1024]{1,0:T(8,128)(2,1)S(1)} %copy-done), kind=kOutput, calls=%fused_computation.1 | convolution fusion | flops 940048384 | bytes 3801088 | tf_op jit(solution)/shard_map/dot_general | solution.py:73
  39.7 7.8 %all-to-all-start = ((bf16[16,32,1024]{2,1,0:T(8,128)(2,1)}), bf16[16,32,1024]{2,1,0:T(8,128)(2,1)S(1)}, u32[]{:S(2)}, u32[]{:S(2)}) async-start(bf16[16,32,1024]{2,1,0:T(8,128)(2,1)} %bitcast.63), calls=%async_computation | async-start | bytes 2097152 | tf_op jit(solution)/shard_map/all_to_all | solution.py:35
  47.5 3.4 %collective-permute-start = (bf16[4,32,1024]{2,1,0:T(8,128)(2,1)S(1)}, bf16[4,32,1024]{2,1,0:T(8,128)(2,1)}, u32[]{:S(2)}, u32[]{:S(2)}) collective-permute-start(bf16[4,32,1024]{2,1,0:T(8,128)(2,1)S(1)} %bitcast.59), channel_id=1, source_target_pairs={{0,4},{4,8},{8,12},{12,16},{16,20},{20,24},{24,28},{28,32},{32,36}... | collective-permute-start | bytes 786440 | tf_op jit(solution)/shard_map/ppermute | solution.py:11
  50.9 2.5 %collective-permute-start.1 = (bf16[4,32,1024]{2,1,0:T(8,128)(2,1)S(1)}, bf16[4,32,1024]{2,1,0:T(8,128)(2,1)}, u32[]{:S(2)}, u32[]{:S(2)}) collective-permute-start(bf16[4,32,1024]{2,1,0:T(8,128)(2,1)S(1)} %bitcast.60), channel_id=1, source_target_pairs={{0,60},{4,0},{8,4},{12,8},{16,12},{20,16},{24,20},{28,24},{32,28},... | collective-permute-start | bytes 786440 | tf_op jit(solution)/shard_map/ppermute | solution.py:11
  53.3 4.9 %collective-permute-start.2 = (bf16[4,32,1024]{2,1,0:T(8,128)(2,1)S(1)}, bf16[4,32,1024]{2,1,0:T(8,128)(2,1)S(1)}, u32[]{:S(2)}, u32[]{:S(2)}) collective-permute-start(bf16[4,32,1024]{2,1,0:T(8,128)(2,1)S(1)} %bitcast.61), channel_id=1, source_target_pairs={{0,8},{4,12},{8,16},{12,20},{16,24},{20,28},{24,32},{28,36},{32,40... | collective-permute-start | bytes 786440 | tf_op jit(solution)/shard_map/ppermute | solution.py:11
  58.3 41.7 %collective-permute-done = bf16[4,32,1024]{2,1,0:T(8,128)(2,1)} collective-permute-done((bf16[4,32,1024]{2,1,0:T(8,128)(2,1)S(1)}, bf16[4,32,1024]{2,1,0:T(8,128)(2,1)}, u32[]{:S(2)}, u32[]{:S(2)}) %collective-permute-start) | collective-permute-done | bytes 262176 | tf_op jit(solution)/shard_map/ppermute | solution.py:11
  102.1 10.8 %collective-permute-done.2 = bf16[4,32,1024]{2,1,0:T(8,128)(2,1)S(1)} collective-permute-done((bf16[4,32,1024]{2,1,0:T(8,128)(2,1)S(1)}, bf16[4,32,1024]{2,1,0:T(8,128)(2,1)S(1)}, u32[]{:S(2)}, u32[]{:S(2)}) %collective-permute-start.2) | collective-permute-done | bytes 262176 | tf_op jit(solution)/shard_map/ppermute | solution.py:11
  113.0 2.4 %multiply_convert_fusion = bf16[896,1024]{1,0:T(8,128)(2,1)} fusion(bf16[512,896]{1,0:T(8,128)(2,1)S(1)} %copy-done.2, bf16[512,1024]{1,0:T(8,128)(2,1)S(1)} %bitcast.64), kind=kOutput, calls=%fused_computation | convolution fusion | flops 941359104 | bytes 3801088 | tf_op jit(solution)/shard_map/dot_general | solution.py:79
  115.4 1.3 convolution_convert_fusion.1
  117.6 1.9 %collective-permute-start.3 = (bf16[2,128,896]{2,1,0:T(8,128)(2,1)S(1)}, bf16[2,128,896]{2,1,0:T(8,128)(2,1)}, u32[]{:S(2)}, u32[]{:S(2)}) collective-permute-start(bf16[2,128,896]{2,1,0:T(8,128)(2,1)S(1)} %dynamic-slice_bitcast_fusion), channel_id=1, source_target_pairs={{0,1},{1,0},{2,3},{3,2},{4,5},{5,4},{6,7},{7,6},{8,9},{9,8},{10,11... | collective-permute-start | bytes 1376264 | tf_op jit(solution)/shard_map/ppermute | solution.py:57
  119.6 2.7 %dynamic-slice_bitcast_fusion.7 = (bf16[112,1024]{1,0:T(8,128)(2,1)}, bf16[112,1024]{1,0:T(8,128)(2,1)}, bf16[112,1024]{1,0:T(8,128)(2,1)}, bf16[112,1024]{1,0:T...) fusion(bf16[8,112,1024]{2,1,0:T(8,128)(2,1)} %bitcast.57, ...), kind=kLoop, calls=%fused_computation.39 | loop fusion | bytes 3211292 | tf_op jit(solution)/shard_map/jit(dynamic_index_in_dim)/squeeze | solution.py:15
  122.3 3.5 %collective-permute-start.5 = (bf16[112,1024]{1,0:T(8,128)(2,1)}, bf16[112,1024]{1,0:T(8,128)(2,1)}, u32[]{:S(2)}, u32[]{:S(2)}) collective-permute-start(bf16[112,1024]{1,0:T(8,128)(2,1)} %get-tuple-element.16), channel_id=1, source_target_pairs={{0,128},{64,192},{128,256},{192,320},{256,384},{320,448},{384,0},{... | collective-permute-start | bytes 688136 | tf_op jit(solution)/shard_map/ppermute | solution.py:47
  125.7 7.0 %collective-permute-start.11 = (bf16[112,1024]{1,0:T(8,128)(2,1)}, bf16[112,1024]{1,0:T(8,128)(2,1)}, u32[]{:S(2)}, u32[]{:S(2)}) collective-permute-start(bf16[112,1024]{1,0:T(8,128)(2,1)} %get-tuple-element.17), channel_id=1, source_target_pairs={{0,320},{64,256},{128,448},{192,384},{256,64},{320,0},{384,192},{4... | collective-permute-start | bytes 688136 | tf_op jit(solution)/shard_map/ppermute | solution.py:47
  132.7 2.5 %collective-permute-start.10 = (bf16[112,1024]{1,0:T(8,128)(2,1)}, bf16[112,1024]{1,0:T(8,128)(2,1)S(1)}, u32[]{:S(2)}, u32[]{:S(2)}) collective-permute-start(bf16[112,1024]{1,0:T(8,128)(2,1)} %get-tuple-element.18), channel_id=1, source_target_pairs={{0,256},{64,320},{128,384},{192,448},{256,0},{320,64},{384,128},{4... | collective-permute-start | bytes 688136 | tf_op jit(solution)/shard_map/ppermute | solution.py:47
  135.3 3.8 %collective-permute-start.9 = (bf16[112,1024]{1,0:T(8,128)(2,1)}, bf16[112,1024]{1,0:T(8,128)(2,1)S(1)}, u32[]{:S(2)}, u32[]{:S(2)}) collective-permute-start(bf16[112,1024]{1,0:T(8,128)(2,1)} %get-tuple-element.19), channel_id=1, source_target_pairs={{0,448},{64,384},{128,64},{192,0},{256,192},{320,128},{384,320},{4... | collective-permute-start | bytes 688136 | tf_op jit(solution)/shard_map/ppermute | solution.py:47
  139.1 4.4 %collective-permute-start.8 = (bf16[112,1024]{1,0:T(8,128)(2,1)}, bf16[112,1024]{1,0:T(8,128)(2,1)S(1)}, u32[]{:S(2)}, u32[]{:S(2)}) collective-permute-start(bf16[112,1024]{1,0:T(8,128)(2,1)} %get-tuple-element.20), channel_id=1, source_target_pairs={{0,192},{64,128},{128,320},{192,256},{256,448},{320,384},{384,64},... | collective-permute-start | bytes 688136 | tf_op jit(solution)/shard_map/ppermute | solution.py:47
  143.6 2.7 %collective-permute-start.7 = (bf16[112,1024]{1,0:T(8,128)(2,1)}, bf16[112,1024]{1,0:T(8,128)(2,1)S(1)}, u32[]{:S(2)}, u32[]{:S(2)}) collective-permute-start(bf16[112,1024]{1,0:T(8,128)(2,1)} %get-tuple-element.21), channel_id=1, source_target_pairs={{0,64},{64,0},{128,192},{192,128},{256,320},{320,256},{384,448},{4... | collective-permute-start | bytes 688136 | tf_op jit(solution)/shard_map/ppermute | solution.py:47
  146.3 4.8 %collective-permute-start.6 = (bf16[112,1024]{1,0:T(8,128)(2,1)}, bf16[112,1024]{1,0:T(8,128)(2,1)S(1)}, u32[]{:S(2)}, u32[]{:S(2)}) collective-permute-start(bf16[112,1024]{1,0:T(8,128)(2,1)} %get-tuple-element.22), channel_id=1, source_target_pairs={{0,384},{64,448},{128,0},{192,64},{256,128},{320,192},{384,256},{4... | collective-permute-start | bytes 688136 | tf_op jit(solution)/shard_map/ppermute | solution.py:47
  152.4 2.6 %collective-permute-start.4 = (bf16[128,896]{1,0:T(8,128)(2,1)S(1)}, bf16[128,896]{1,0:T(8,128)(2,1)S(1)}, u32[]{:S(2)}, u32[]{:S(2)}) collective-permute-start(bf16[128,896]{1,0:T(8,128)(2,1)S(1)} %fusion.14), channel_id=1, source_target_pairs={{0,2},{1,3},{2,0},{3,1},{4,6},{5,7},{6,4},{7,5},{8,10},{9,11},{10,... | collective-permute-start | bytes 688136 | tf_op jit(solution)/shard_map/ppermute | solution.py:59
  155.0 2.0 %collective-permute-done.7 = bf16[112,1024]{1,0:T(8,128)(2,1)S(1)} collective-permute-done((bf16[112,1024]{1,0:T(8,128)(2,1)}, bf16[112,1024]{1,0:T(8,128)(2,1)S(1)}, u32[]{:S(2)}, u32[]{:S(2)}) %collective-permute-start.7) | collective-permute-done | bytes 229408 | tf_op jit(solution)/shard_map/ppermute | solution.py:47
  157.1 2.2 %fusion.13 = f32[112,1024]{1,0:T(8,128)} fusion(bf16[112,1024]{1,0:T(8,128)(2,1)} %collective-permute-done.11, bf16[112,1024]{1,0:T(8,128)(2,1)S(1)} %collective-permute-done.10, bf16[112,1024]{1,0:T(8,128)(2,1)S(1)} %collective-permute-done.9, bf16[112,1024]{1,0:T(8,128)(2,1)S(1)} %collective-permute-done.8, ...), kind=kLoop, calls=%fused_computation.23 | loop fusion | flops 1720320 | bytes 2293764 | tf_op jit(solution)/shard_map/add | solution.py:47
  159.3 1.3 collective-permute-done.4
  (32 shorter events, 7.5 us)
Async XLA Ops:
  0.6 36.9 %copy-start = (bf16[896,1024]{1,0:T(8,128)(2,1)S(1)}, bf16[896,1024]{1,0:T(8,128)(2,1)}, u32[]{:S(2)}) copy-start(bf16[896,1024]{1,0:T(8,128)(2,1)} %param.7) | copy-start | bytes 5505028
  37.5 2.3 %copy-start.1 = (bf16[512,896]{1,0:T(8,128)(2,1)}, bf16[512,896]{1,0:T(8,128)(2,1)S(1)}, u32[]{:S(2)}) copy-start(bf16[512,896]{1,0:T(8,128)(2,1)S(1)} %all_gather.11) | copy-start | bytes 2752516
  39.7 121.8 %all-to-all-start = ((bf16[16,32,1024]{2,1,0:T(8,128)(2,1)}), bf16[16,32,1024]{2,1,0:T(8,128)(2,1)S(1)}, u32[]{:S(2)}, u32[]{:S(2)}) async-start(bf16[16,32,1024]{2,1,0:T(8,128)(2,1)} %bitcast.63), calls=%async_computation | async-start | bytes 2097152 | tf_op jit(solution)/shard_map/all_to_all | solution.py:35
  47.5 52.5 %collective-permute-start = (bf16[4,32,1024]{2,1,0:T(8,128)(2,1)S(1)}, bf16[4,32,1024]{2,1,0:T(8,128)(2,1)}, u32[]{:S(2)}, u32[]{:S(2)}) collective-permute-start(bf16[4,32,1024]{2,1,0:T(8,128)(2,1)S(1)} %bitcast.59), channel_id=1, source_target_pairs={{0,4},{4,8},{8,12},{12,16},{16,20},{20,24},{24,28},{28,32},{32,36}... | collective-permute-start | bytes 786440 | tf_op jit(solution)/shard_map/ppermute | solution.py:11
  50.9 50.3 %collective-permute-start.1 = (bf16[4,32,1024]{2,1,0:T(8,128)(2,1)S(1)}, bf16[4,32,1024]{2,1,0:T(8,128)(2,1)}, u32[]{:S(2)}, u32[]{:S(2)}) collective-permute-start(bf16[4,32,1024]{2,1,0:T(8,128)(2,1)S(1)} %bitcast.60), channel_id=1, source_target_pairs={{0,60},{4,0},{8,4},{12,8},{16,12},{20,16},{24,20},{28,24},{32,28},... | collective-permute-start | bytes 786440 | tf_op jit(solution)/shard_map/ppermute | solution.py:11
  53.3 59.6 %collective-permute-start.2 = (bf16[4,32,1024]{2,1,0:T(8,128)(2,1)S(1)}, bf16[4,32,1024]{2,1,0:T(8,128)(2,1)S(1)}, u32[]{:S(2)}, u32[]{:S(2)}) collective-permute-start(bf16[4,32,1024]{2,1,0:T(8,128)(2,1)S(1)} %bitcast.61), channel_id=1, source_target_pairs={{0,8},{4,12},{8,16},{12,20},{16,24},{20,28},{24,32},{28,36},{32,40... | collective-permute-start | bytes 786440 | tf_op jit(solution)/shard_map/ppermute | solution.py:11
  58.3 54.7 %copy-start.2 = (bf16[512,896]{1,0:T(8,128)(2,1)S(1)}, bf16[512,896]{1,0:T(8,128)(2,1)}, u32[]{:S(2)}) copy-start(bf16[512,896]{1,0:T(8,128)(2,1)} %copy-done.1) | copy-start | bytes 2752516
  116.7 0.9 copy-start.3
  117.6 28.6 %collective-permute-start.3 = (bf16[2,128,896]{2,1,0:T(8,128)(2,1)S(1)}, bf16[2,128,896]{2,1,0:T(8,128)(2,1)}, u32[]{:S(2)}, u32[]{:S(2)}) collective-permute-start(bf16[2,128,896]{2,1,0:T(8,128)(2,1)S(1)} %dynamic-slice_bitcast_fusion), channel_id=1, source_target_pairs={{0,1},{1,0},{2,3},{3,2},{4,5},{5,4},{6,7},{7,6},{8,9},{9,8},{10,11... | collective-permute-start | bytes 1376264 | tf_op jit(solution)/shard_map/ppermute | solution.py:57
  122.3 16.8 %collective-permute-start.5 = (bf16[112,1024]{1,0:T(8,128)(2,1)}, bf16[112,1024]{1,0:T(8,128)(2,1)}, u32[]{:S(2)}, u32[]{:S(2)}) collective-permute-start(bf16[112,1024]{1,0:T(8,128)(2,1)} %get-tuple-element.16), channel_id=1, source_target_pairs={{0,128},{64,192},{128,256},{192,320},{256,384},{320,448},{384,0},{... | collective-permute-start | bytes 688136 | tf_op jit(solution)/shard_map/ppermute | solution.py:47
  125.7 17.8 %collective-permute-start.11 = (bf16[112,1024]{1,0:T(8,128)(2,1)}, bf16[112,1024]{1,0:T(8,128)(2,1)}, u32[]{:S(2)}, u32[]{:S(2)}) collective-permute-start(bf16[112,1024]{1,0:T(8,128)(2,1)} %get-tuple-element.17), channel_id=1, source_target_pairs={{0,320},{64,256},{128,448},{192,384},{256,64},{320,0},{384,192},{4... | collective-permute-start | bytes 688136 | tf_op jit(solution)/shard_map/ppermute | solution.py:47
  132.7 19.7 %collective-permute-start.10 = (bf16[112,1024]{1,0:T(8,128)(2,1)}, bf16[112,1024]{1,0:T(8,128)(2,1)S(1)}, u32[]{:S(2)}, u32[]{:S(2)}) collective-permute-start(bf16[112,1024]{1,0:T(8,128)(2,1)} %get-tuple-element.18), channel_id=1, source_target_pairs={{0,256},{64,320},{128,384},{192,448},{256,0},{320,64},{384,128},{4... | collective-permute-start | bytes 688136 | tf_op jit(solution)/shard_map/ppermute | solution.py:47
  135.3 19.7 %collective-permute-start.9 = (bf16[112,1024]{1,0:T(8,128)(2,1)}, bf16[112,1024]{1,0:T(8,128)(2,1)S(1)}, u32[]{:S(2)}, u32[]{:S(2)}) collective-permute-start(bf16[112,1024]{1,0:T(8,128)(2,1)} %get-tuple-element.19), channel_id=1, source_target_pairs={{0,448},{64,384},{128,64},{192,0},{256,192},{320,128},{384,320},{4... | collective-permute-start | bytes 688136 | tf_op jit(solution)/shard_map/ppermute | solution.py:47
  139.1 15.9 %collective-permute-start.8 = (bf16[112,1024]{1,0:T(8,128)(2,1)}, bf16[112,1024]{1,0:T(8,128)(2,1)S(1)}, u32[]{:S(2)}, u32[]{:S(2)}) collective-permute-start(bf16[112,1024]{1,0:T(8,128)(2,1)} %get-tuple-element.20), channel_id=1, source_target_pairs={{0,192},{64,128},{128,320},{192,256},{256,448},{320,384},{384,64},... | collective-permute-start | bytes 688136 | tf_op jit(solution)/shard_map/ppermute | solution.py:47
  143.6 13.5 %collective-permute-start.7 = (bf16[112,1024]{1,0:T(8,128)(2,1)}, bf16[112,1024]{1,0:T(8,128)(2,1)S(1)}, u32[]{:S(2)}, u32[]{:S(2)}) collective-permute-start(bf16[112,1024]{1,0:T(8,128)(2,1)} %get-tuple-element.21), channel_id=1, source_target_pairs={{0,64},{64,0},{128,192},{192,128},{256,320},{320,256},{384,448},{4... | collective-permute-start | bytes 688136 | tf_op jit(solution)/shard_map/ppermute | solution.py:47
  146.3 10.8 %collective-permute-start.6 = (bf16[112,1024]{1,0:T(8,128)(2,1)}, bf16[112,1024]{1,0:T(8,128)(2,1)S(1)}, u32[]{:S(2)}, u32[]{:S(2)}) collective-permute-start(bf16[112,1024]{1,0:T(8,128)(2,1)} %get-tuple-element.22), channel_id=1, source_target_pairs={{0,384},{64,448},{128,0},{192,64},{256,128},{320,192},{384,256},{4... | collective-permute-start | bytes 688136 | tf_op jit(solution)/shard_map/ppermute | solution.py:47
  152.3 8.2 %copy-start.4 = (bf16[128,896]{1,0:T(8,128)(2,1)S(1)}, bf16[128,896]{1,0:T(8,128)(2,1)}, u32[]{:S(2)}) copy-start(bf16[128,896]{1,0:T(8,128)(2,1)} %param.5) | copy-start | bytes 688132
  152.3 8.2 %copy-start.5 = (bf16[128,896]{1,0:T(8,128)(2,1)S(1)}, bf16[128,896]{1,0:T(8,128)(2,1)}, u32[]{:S(2)}) copy-start(bf16[128,896]{1,0:T(8,128)(2,1)} %param.4) | copy-start | bytes 688132
  152.4 8.1 %collective-permute-start.4 = (bf16[128,896]{1,0:T(8,128)(2,1)S(1)}, bf16[128,896]{1,0:T(8,128)(2,1)S(1)}, u32[]{:S(2)}, u32[]{:S(2)}) collective-permute-start(bf16[128,896]{1,0:T(8,128)(2,1)S(1)} %fusion.14), channel_id=1, source_target_pairs={{0,2},{1,3},{2,0},{3,1},{4,6},{5,7},{6,4},{7,5},{8,10},{9,11},{10,... | collective-permute-start | bytes 688136 | tf_op jit(solution)/shard_map/ppermute | solution.py:59
where the time goes:
time: 163 us; the launch traced here: 162 us
  waiting for transfers between devices  55.8 us (34%)
  starting transfers between devices  51.7 us (32%)
  blocking collectives  35.6 us (22%)
  other arithmetic  6.52 us (4%)
  matrix products  5.95 us (4%)
  local copies, waits for them, and re-layouts  5.8 us (4%)
    ppermute x3, waiting for transfers between devices, shifted(): lax.ppermute(array, axis, [(i, (i + by) % count) for i in range(count)])  52.5 us
    ppermute x7, starting transfers between devices, sum_over_dp(): total = total + lax.ppermute(mine, 'dp', route).astype(jnp.float32)  28.7 us
    all_gather x1, blocking collectives, gather_apart(): lax.all_gather(block, 'row', axis=0, tiled=False, axis_index_groups=groups)  26.3 us
    ppermute x3, starting transfers between devices, shifted(): lax.ppermute(array, axis, [(i, (i + by) % count) for i in range(count)])  10.8 us
    all_gather x1, blocking collectives, shards(): hidden_all = lax.all_gather(hidden, 'col', axis=0, tiled=True)  9.31 us
    all_to_all x1, starting transfers between devices, sum_over_row(): parts = lax.all_to_all(parts, 'row', 0, 0, tiled=True)  7.76 us
  transfers between devices with their start and end apart: 13, of which 4 were waited for; matrix products, arithmetic and copies ran while one was open for 8% of the time, Pallas kernels for 0%

commit v1 on v0

--- a/solution.py
+++ b/solution.py
@@ -22,11 +22,11 @@
 
 def gather_near(same):
     low = lax.axis_index("row") & 3
-    whole = jnp.zeros((4,) + same.shape, same.dtype)
-    for by in (1, 15, 2, 0):
-        got = same if by == 0 else shifted(same, "row", by)
-        whole = lax.dynamic_update_slice(whole, got[:, None], (0, (low - by) & 3, 0, 0))
-    return whole.reshape(-1, same.shape[-1])
+    sets = [same]
+    for by in (1, 2, 15):
+        sets.append(shifted(same, "row", by))
+    whole = [lax.select_n((low - k) & 3, *sets) for k in range(4)]
+    return jnp.stack(whole, axis=1).reshape(-1, same.shape[-1])
 
 
 def sum_over_row(parts):
@@ -37,15 +37,17 @@
 
 
 def sum_over_dp(parts):
-    parts = parts.reshape((8, parts.shape[0] // 8) + parts.shape[1:])
+    parts = parts.reshape((4, 2, parts.shape[0] // 8) + parts.shape[1:])
     me = lax.axis_index("dp")
     y, x = me >> 1, me & 1
-    total = pick(parts, me).astype(jnp.float32)
-    for dy, dx in ((1, 0), (3, 0), (0, 1), (1, 1), (3, 1), (2, 0), (2, 1)):
-        route = [(a * 2 + b, (a + dy) % 4 * 2 + (b + dx) % 2) for a in range(4) for b in range(2)]
-        mine = pick(parts, ((y + dy) & 3) * 2 + ((x + dx) & 1))
-        total = total + lax.ppermute(mine, "dp", route).astype(jnp.float32)
-    return total
+    own, *blocks = hold([pick(parts, (y + dy) & 3) for dy in (0, 2, 1, 3)])
+    total = own.astype(jnp.float32)
+    for dy, mine in zip((2, 1, 3), blocks):
+        got = lax.ppermute(mine, "dp", [(i, (i + 2 * dy) % 8) for i in range(8)])
+        total = total + got.astype(jnp.float32)
+    away = pick(total, 1 - x).astype(jnp.bfloat16)
+    away = lax.ppermute(away, "dp", [(i, i ^ 1) for i in range(8)])
+    return pick(total, x) + away.astype(jnp.float32)
 
 
 def sum_over_col(parts):
@@ -54,22 +56,29 @@
     x, core = me >> 1, me & 1
     other = lax.dynamic_index_in_dim(parts, 1 - core, 1, keepdims=False)
     mine = lax.dynamic_index_in_dim(parts, core, 1, keepdims=False)
+    other, mine = hold((other, mine))
     other = lax.ppermute(other, "col", [(i, i ^ 1) for i in range(4)])
     pair = mine.astype(jnp.float32) + other.astype(jnp.float32)
-    away = lax.ppermute(pick(pair, 1 - x).astype(jnp.bfloat16), "col", [(i, i ^ 2) for i in range(4)])
+    away = pick(pair, 1 - x).astype(jnp.bfloat16)
+    away = lax.ppermute(away, "col", [(i, i ^ 2) for i in range(4)])
     return pick(pair, x) + away.astype(jnp.float32)
 
 
 def shards(gate_pre, up_pre, out_grad, down_weight):
-    grad_apart = gather_apart(out_grad)
-
     gate32 = gate_pre.astype(jnp.float32)
     up32 = up_pre.astype(jnp.float32)
     sgate = jax.nn.sigmoid(gate32)
     act = gate32 * sgate
-    hidden, grad_apart = hold(((act * up32).astype(jnp.bfloat16), grad_apart))
+    hidden = hold((act * up32).astype(jnp.bfloat16))
+    me = lax.axis_index("col")
+    ahead = lax.ppermute(hidden, "col", [(i, i ^ 2) for i in range(4)])
+    grad_apart = gather_apart(out_grad)
     grad_all = gather_near(grad_apart)
-    hidden_all = lax.all_gather(hidden, "col", axis=0, tiled=True)
+    ahead, grad_late = hold((ahead, grad_apart))
+    pair = jnp.stack([lax.select_n(me >> 1, hidden, ahead), lax.select_n(me >> 1, ahead, hidden)])
+    beside = lax.ppermute(pair, "col", [(i, i ^ 1) for i in range(4)])
+    hidden_all = jnp.stack([lax.select_n(me & 1, pair, beside), lax.select_n(me & 1, beside, pair)], axis=1)
+    hidden_all = hidden_all.reshape(-1, hidden.shape[1])
     layer_parts = jnp.dot(hidden_all, down_weight, preferred_element_type=jnp.float32).astype(jnp.bfloat16)
     layer_out = sum_over_row(layer_parts).astype(jnp.bfloat16)
 
@@ -83,11 +92,10 @@
     ).astype(jnp.bfloat16)
     local_grad, grad_late = hold((local_grad, grad_all))
     weight_grad = sum_over_dp(local_grad)
-    dhidden = sum_over_col(
-        lax.dot_general(
-            grad_late, down_weight, (((1,), (1,)), ((), ())), preferred_element_type=jnp.float32
-        ).astype(jnp.bfloat16)
-    )
+    back = lax.dot_general(
+        grad_late, down_weight, (((1,), (1,)), ((), ())), preferred_element_type=jnp.float32
+    ).astype(jnp.bfloat16)
+    dhidden = sum_over_col(back)
     up_grad = (dhidden * act).astype(jnp.bfloat16)
     gate_grad = (dhidden * up32 * sgate * (1.0 + gate32 * (1.0 - sgate))).astype(jnp.bfloat16)
     return (layer_out, gate_grad, up_grad, weight_grad)

time: 163 us -> 163 us (level)
  the two profiles are of different devices: /device:TPU:32 before, /device:TPU:2 now
where the time goes in v1:
time: 163 us; the launch traced here: 162 us
  waiting for transfers between devices  75.5 us (46%)
  starting transfers between devices  48 us (29%)
  blocking collectives  21.4 us (13%)
  other arithmetic  9.43 us (6%)
  matrix products  4.71 us (3%)
  local copies, waits for them, and re-layouts  2.24 us (1%)
    ppermute x3, waiting for transfers between devices, shifted(): lax.ppermute(array, axis, [(i, (i + by) % count) for i in range(count)])  55.1 us
    all_gather x1, blocking collectives, gather_apart(): lax.all_gather(block, 'row', axis=0, tiled=False, axis_index_groups=groups)  21.4 us
    ppermute x3, waiting for transfers between devices, sum_over_dp(): got = lax.ppermute(mine, 'dp', [(i, (i + 2 * dy) % 8) for i in range(8)])  14.4 us
    ppermute x3, starting transfers between devices, sum_over_dp(): got = lax.ppermute(mine, 'dp', [(i, (i + 2 * dy) % 8) for i in range(8)])  10.9 us
    ppermute x3, starting transfers between devices, shifted(): lax.ppermute(array, axis, [(i, (i + by) % count) for i in range(count)])  10.6 us
    ppermute x1, starting transfers between devices, shards(): ahead = lax.ppermute(hidden, 'col', [(i, i ^ 2) for i in range(4)])  7.79 us
    all_to_all x1, starting transfers between devices, sum_over_row(): parts = lax.all_to_all(parts, 'row', 0, 0, tiled=True)  6.75 us
    ppermute x1, starting transfers between devices, sum_over_dp(): away = lax.ppermute(away, 'dp', [(i, i ^ 1) for i in range(8)])  4.46 us
  transfers between devices with their start and end apart: 12, of which 7 were waited for; matrix products, arithmetic and copies ran while one was open for 7% of the time, Pallas kernels for 0%

profile of v1, /device:TPU:2, one launch (start us, length us, event | category | flops | bytes accessed | tf_op | source)
XLA Modules:
  0.0 162.3 jit_solution(14455027356146845310)
XLA Ops:
  0.6 1.3 fusion
  2.0 7.8 %collective-permute-start = (bf16[128,896]{1,0:T(8,128)(2,1)S(1)}, bf16[128,896]{1,0:T(8,128)(2,1)S(1)}, u32[]{:S(2)}, u32[]{:S(2)}) collective-permute-start(bf16[128,896]{1,0:T(8,128)(2,1)S(1)} %fusion), channel_id=1, source_target_pairs={{0,2},{1,3},{2,0},{3,1},{4,6},{5,7},{6,4},{7,5},{8,10},{9,11},{10,... | collective-permute-start | bytes 688136 | tf_op jit(solution)/shard_map/ppermute | solution.py:74
  9.8 21.4 %all-gather = bf16[128,1024]{1,0:T(8,128)(2,1)S(1)} all-gather(bf16[32,1024]{1,0:T(8,128)(2,1)} %param.6), channel_id=2, replica_groups={{0,16,32,48},{4,20,36,52},{8,24,40,56},{12,28,44,60},{1,17,33,49},{5,21..., dimensions={0}, use_global_device_ids=true | all-gather | bytes 327680 | tf_op jit(solution)/shard_map/all_gather | solution.py:20
  31.3 1.9 %collective-permute-start.1 = (bf16[2,128,896]{2,1,0:T(8,128)(2,1)S(1)}, bf16[2,128,896]{2,1,0:T(8,128)(2,1)}, u32[]{:S(2)}, u32[]{:S(2)}) collective-permute-start(bf16[2,128,896]{2,1,0:T(8,128)(2,1)S(1)} %pad_maximum_fusion.2), channel_id=1, source_target_pairs={{0,1},{1,0},{2,3},{3,2},{4,5},{5,4},{6,7},{7,6},{8,9},{9,8},{10,11... | collective-permute-start | bytes 1376264 | tf_op jit(solution)/shard_map/ppermute | solution.py:79
  33.2 1.9 %collective-permute-done.1 = bf16[2,128,896]{2,1,0:T(8,128)(2,1)} collective-permute-done((bf16[2,128,896]{2,1,0:T(8,128)(2,1)S(1)}, bf16[2,128,896]{2,1,0:T(8,128)(2,1)}, u32[]{:S(2)}, u32[]{:S(2)}) %collective-permute-start.1) | collective-permute-done | bytes 458784 | tf_op jit(solution)/shard_map/ppermute | solution.py:79
  36.4 2.3 %convolution_convert_fusion = bf16[512,1024]{1,0:T(8,128)(2,1)} fusion(bf16[512,896]{1,0:T(8,128)(2,1)S(1)} %bitcast.68, bf16[896,1024]{1,0:T(8,128)(2,1)S(1)} %copy-done), kind=kOutput, calls=%fused_computation.1 | convolution fusion | flops 940048384 | bytes 3801088 | tf_op jit(solution)/shard_map/dot_general | solution.py:82
  38.6 6.8 %all-to-all-start = ((bf16[16,32,1024]{2,1,0:T(8,128)(2,1)}), bf16[16,32,1024]{2,1,0:T(8,128)(2,1)S(1)}, u32[]{:S(2)}, u32[]{:S(2)}) async-start(bf16[16,32,1024]{2,1,0:T(8,128)(2,1)} %bitcast.65), calls=%async_computation | async-start | bytes 2097152 | tf_op jit(solution)/shard_map/all_to_all | solution.py:35
  45.4 4.7 %collective-permute-start.3 = (bf16[4,32,1024]{2,1,0:T(8,128)(2,1)S(1)}, bf16[4,32,1024]{2,1,0:T(8,128)(2,1)S(1)}, u32[]{:S(2)}, u32[]{:S(2)}) collective-permute-start(bf16[4,32,1024]{2,1,0:T(8,128)(2,1)S(1)} %bitcast.61), channel_id=1, source_target_pairs={{0,8},{4,12},{8,16},{12,20},{16,24},{20,28},{24,32},{28,36},{32,40... | collective-permute-start | bytes 786440 | tf_op jit(solution)/shard_map/ppermute | solution.py:11
  50.1 3.7 %collective-permute-start.4 = (bf16[4,32,1024]{2,1,0:T(8,128)(2,1)S(1)}, bf16[4,32,1024]{2,1,0:T(8,128)(2,1)}, u32[]{:S(2)}, u32[]{:S(2)}) collective-permute-start(bf16[4,32,1024]{2,1,0:T(8,128)(2,1)S(1)} %bitcast.62), channel_id=1, source_target_pairs={{0,60},{4,0},{8,4},{12,8},{16,12},{20,16},{24,20},{28,24},{32,28},... | collective-permute-start | bytes 786440 | tf_op jit(solution)/shard_map/ppermute | solution.py:11
  53.8 2.2 %collective-permute-start.2 = (bf16[4,32,1024]{2,1,0:T(8,128)(2,1)S(1)}, bf16[4,32,1024]{2,1,0:T(8,128)(2,1)}, u32[]{:S(2)}, u32[]{:S(2)}) collective-permute-start(bf16[4,32,1024]{2,1,0:T(8,128)(2,1)S(1)} %bitcast.63), channel_id=1, source_target_pairs={{0,4},{4,8},{8,12},{12,16},{16,20},{20,24},{24,28},{28,32},{32,36}... | collective-permute-start | bytes 786440 | tf_op jit(solution)/shard_map/ppermute | solution.py:11
  56.0 50.3 %collective-permute-done.3 = bf16[4,32,1024]{2,1,0:T(8,128)(2,1)S(1)} collective-permute-done((bf16[4,32,1024]{2,1,0:T(8,128)(2,1)S(1)}, bf16[4,32,1024]{2,1,0:T(8,128)(2,1)S(1)}, u32[]{:S(2)}, u32[]{:S(2)}) %collective-permute-start.3) | collective-permute-done | bytes 262176 | tf_op jit(solution)/shard_map/ppermute | solution.py:11
  106.4 4.8 %collective-permute-done.2 = bf16[4,32,1024]{2,1,0:T(8,128)(2,1)} collective-permute-done((bf16[4,32,1024]{2,1,0:T(8,128)(2,1)S(1)}, bf16[4,32,1024]{2,1,0:T(8,128)(2,1)}, u32[]{:S(2)}, u32[]{:S(2)}) %collective-permute-start.2) | collective-permute-done | bytes 262176 | tf_op jit(solution)/shard_map/ppermute | solution.py:11
  114.9 4.9 %collective-permute-start.9 = (bf16[2,112,1024]{2,1,0:T(8,128)(2,1)}, bf16[2,112,1024]{2,1,0:T(8,128)(2,1)}, u32[]{:S(2)}, u32[]{:S(2)}) collective-permute-start(bf16[2,112,1024]{2,1,0:T(8,128)(2,1)} %get-tuple-element.25), channel_id=1, source_target_pairs={{0,384},{64,448},{128,0},{192,64},{256,128},{320,192},{384,256},{4... | collective-permute-start | bytes 1376264 | tf_op jit(solution)/shard_map/ppermute | solution.py:46
  119.8 1.9 %collective-permute-start.8 = (bf16[2,112,1024]{2,1,0:T(8,128)(2,1)}, bf16[2,112,1024]{2,1,0:T(8,128)(2,1)}, u32[]{:S(2)}, u32[]{:S(2)}) collective-permute-start(bf16[2,112,1024]{2,1,0:T(8,128)(2,1)} %get-tuple-element.24), channel_id=1, source_target_pairs={{0,128},{64,192},{128,256},{192,320},{256,384},{320,448},{384,0},{... | collective-permute-start | bytes 1376264 | tf_op jit(solution)/shard_map/ppermute | solution.py:46
  121.7 4.1 %collective-permute-start.7 = (bf16[2,112,1024]{2,1,0:T(8,128)(2,1)}, bf16[2,112,1024]{2,1,0:T(8,128)(2,1)}, u32[]{:S(2)}, u32[]{:S(2)}) collective-permute-start(bf16[2,112,1024]{2,1,0:T(8,128)(2,1)} %get-tuple-element.23), channel_id=1, source_target_pairs={{0,256},{64,320},{128,384},{192,448},{256,0},{320,64},{384,128},{4... | collective-permute-start | bytes 1376264 | tf_op jit(solution)/shard_map/ppermute | solution.py:46
  125.8 1.3 convolution_convert_fusion.1
  128.0 1.9 %collective-permute-start.5 = (bf16[2,128,896]{2,1,0:T(8,128)(2,1)}, bf16[2,128,896]{2,1,0:T(8,128)(2,1)}, u32[]{:S(2)}, u32[]{:S(2)}) collective-permute-start(bf16[2,128,896]{2,1,0:T(8,128)(2,1)} %get-tuple-element.20), channel_id=1, source_target_pairs={{0,1},{1,0},{2,3},{3,2},{4,5},{5,4},{6,7},{7,6},{8,9},{9,8},{10,11... | collective-permute-start | bytes 1376264 | tf_op jit(solution)/shard_map/ppermute | solution.py:60
  129.9 9.1 %collective-permute-done.9 = bf16[2,112,1024]{2,1,0:T(8,128)(2,1)} collective-permute-done((bf16[2,112,1024]{2,1,0:T(8,128)(2,1)}, bf16[2,112,1024]{2,1,0:T(8,128)(2,1)}, u32[]{:S(2)}, u32[]{:S(2)}) %collective-permute-start.9) | collective-permute-done | bytes 458784 | tf_op jit(solution)/shard_map/ppermute | solution.py:46
  139.0 5.3 %collective-permute-done.8 = bf16[2,112,1024]{2,1,0:T(8,128)(2,1)} collective-permute-done((bf16[2,112,1024]{2,1,0:T(8,128)(2,1)}, bf16[2,112,1024]{2,1,0:T(8,128)(2,1)}, u32[]{:S(2)}, u32[]{:S(2)}) %collective-permute-start.8) | collective-permute-done | bytes 458784 | tf_op jit(solution)/shard_map/ppermute | solution.py:46
  144.3 1.7 %convert_add_fusion = f32[2,112,1024]{2,1,0:T(8,128)S(1)} fusion(bf16[2,112,1024]{2,1,0:T(8,128)(2,1)} %collective-permute-done.9, bf16[2,112,1024]{2,1,0:T(8,128)(2,1)} %collective-permute-done.8, bf16[2,112,1024]{2,1,0:T(8,128)(2,1)} %collective-permute-done.7, bf16[2,112,1024]{2,1,0:T(8,128)(2,1)} %get-tuple-element.22), kind=kLoop, calls=%fused_computation.5 | loop fusion | flops 1605632 | bytes 2752512 | tf_op jit(solution)/shard_map/add | solution.py:47
  146.1 4.5 %collective-permute-start.10 = (bf16[112,1024]{1,0:T(8,128)(2,1)S(1)}, bf16[112,1024]{1,0:T(8,128)(2,1)S(1)}, u32[]{:S(2)}, u32[]{:S(2)}) collective-permute-start(bf16[112,1024]{1,0:T(8,128)(2,1)S(1)} %fusion.9), channel_id=1, source_target_pairs={{0,64},{64,0},{128,192},{192,128},{256,320},{320,256},{384,448},{4... | collective-permute-start | bytes 688136 | tf_op jit(solution)/shard_map/ppermute | solution.py:49
  151.8 3.7 %collective-permute-start.6 = (bf16[128,896]{1,0:T(8,128)(2,1)S(1)}, bf16[128,896]{1,0:T(8,128)(2,1)S(1)}, u32[]{:S(2)}, u32[]{:S(2)}) collective-permute-start(bf16[128,896]{1,0:T(8,128)(2,1)S(1)} %fusion.8), channel_id=1, source_target_pairs={{0,2},{1,3},{2,0},{3,1},{4,6},{5,7},{6,4},{7,5},{8,10},{9,11},{10,... | collective-permute-start | bytes 688136 | tf_op jit(solution)/shard_map/ppermute | solution.py:63
  155.5 2.4 %collective-permute-done.10 = bf16[112,1024]{1,0:T(8,128)(2,1)S(1)} collective-permute-done((bf16[112,1024]{1,0:T(8,128)(2,1)S(1)}, bf16[112,1024]{1,0:T(8,128)(2,1)S(1)}, u32[]{:S(2)}, u32[]{:S(2)}) %collective-permute-start.10) | collective-permute-done | bytes 229408 | tf_op jit(solution)/shard_map/ppermute | solution.py:49
  158.7 1.7 %collective-permute-done.6 = bf16[128,896]{1,0:T(8,128)(2,1)S(1)} collective-permute-done((bf16[128,896]{1,0:T(8,128)(2,1)S(1)}, bf16[128,896]{1,0:T(8,128)(2,1)S(1)}, u32[]{:S(2)}, u32[]{:S(2)}) %collective-permute-start.6) | collective-permute-done | bytes 229408 | tf_op jit(solution)/shard_map/ppermute | solution.py:63
  (30 shorter events, 9.8 us)
Async XLA Ops:
  0.6 35.7 %copy-start = (bf16[896,1024]{1,0:T(8,128)(2,1)S(1)}, bf16[896,1024]{1,0:T(8,128)(2,1)}, u32[]{:S(2)}) copy-start(bf16[896,1024]{1,0:T(8,128)(2,1)} %param.7) | copy-start | bytes 5505028
  2.0 29.2 %collective-permute-start = (bf16[128,896]{1,0:T(8,128)(2,1)S(1)}, bf16[128,896]{1,0:T(8,128)(2,1)S(1)}, u32[]{:S(2)}, u32[]{:S(2)}) collective-permute-start(bf16[128,896]{1,0:T(8,128)(2,1)S(1)} %fusion), channel_id=1, source_target_pairs={{0,2},{1,3},{2,0},{3,1},{4,6},{5,7},{6,4},{7,5},{8,10},{9,11},{10,... | collective-permute-start | bytes 688136 | tf_op jit(solution)/shard_map/ppermute | solution.py:74
  31.3 3.8 %collective-permute-start.1 = (bf16[2,128,896]{2,1,0:T(8,128)(2,1)S(1)}, bf16[2,128,896]{2,1,0:T(8,128)(2,1)}, u32[]{:S(2)}, u32[]{:S(2)}) collective-permute-start(bf16[2,128,896]{2,1,0:T(8,128)(2,1)S(1)} %pad_maximum_fusion.2), channel_id=1, source_target_pairs={{0,1},{1,0},{2,3},{3,2},{4,5},{5,4},{6,7},{7,6},{8,9},{9,8},{10,11... | collective-permute-start | bytes 1376264 | tf_op jit(solution)/shard_map/ppermute | solution.py:79
  36.3 2.3 %copy-start.1 = (bf16[2,2,128,896]{3,2,1,0:T(8,128)(2,1)}, bf16[2,2,128,896]{3,2,1,0:T(8,128)(2,1)S(1)}, u32[]{:S(2)}) copy-start(bf16[2,2,128,896]{3,2,1,0:T(8,128)(2,1)S(1)} %pad_maximum_fusion.1) | copy-start | bytes 2752516
  38.6 122.8 %all-to-all-start = ((bf16[16,32,1024]{2,1,0:T(8,128)(2,1)}), bf16[16,32,1024]{2,1,0:T(8,128)(2,1)S(1)}, u32[]{:S(2)}, u32[]{:S(2)}) async-start(bf16[16,32,1024]{2,1,0:T(8,128)(2,1)} %bitcast.65), calls=%async_computation | async-start | bytes 2097152 | tf_op jit(solution)/shard_map/all_to_all | solution.py:35
  45.4 61.0 %collective-permute-start.3 = (bf16[4,32,1024]{2,1,0:T(8,128)(2,1)S(1)}, bf16[4,32,1024]{2,1,0:T(8,128)(2,1)S(1)}, u32[]{:S(2)}, u32[]{:S(2)}) collective-permute-start(bf16[4,32,1024]{2,1,0:T(8,128)(2,1)S(1)} %bitcast.61), channel_id=1, source_target_pairs={{0,8},{4,12},{8,16},{12,20},{16,24},{20,28},{24,32},{28,36},{32,40... | collective-permute-start | bytes 786440 | tf_op jit(solution)/shard_map/ppermute | solution.py:11
  50.1 56.2 %collective-permute-start.4 = (bf16[4,32,1024]{2,1,0:T(8,128)(2,1)S(1)}, bf16[4,32,1024]{2,1,0:T(8,128)(2,1)}, u32[]{:S(2)}, u32[]{:S(2)}) collective-permute-start(bf16[4,32,1024]{2,1,0:T(8,128)(2,1)S(1)} %bitcast.62), channel_id=1, source_target_pairs={{0,60},{4,0},{8,4},{12,8},{16,12},{20,16},{24,20},{28,24},{32,28},... | collective-permute-start | bytes 786440 | tf_op jit(solution)/shard_map/ppermute | solution.py:11
  53.8 57.3 %collective-permute-start.2 = (bf16[4,32,1024]{2,1,0:T(8,128)(2,1)S(1)}, bf16[4,32,1024]{2,1,0:T(8,128)(2,1)}, u32[]{:S(2)}, u32[]{:S(2)}) collective-permute-start(bf16[4,32,1024]{2,1,0:T(8,128)(2,1)S(1)} %bitcast.63), channel_id=1, source_target_pairs={{0,4},{4,8},{8,12},{12,16},{16,20},{20,24},{24,28},{28,32},{32,36}... | collective-permute-start | bytes 786440 | tf_op jit(solution)/shard_map/ppermute | solution.py:11
  56.0 56.4 %copy-start.2 = (bf16[2,2,128,896]{3,2,1,0:T(8,128)(2,1)S(1)}, bf16[2,2,128,896]{3,2,1,0:T(8,128)(2,1)}, u32[]{:S(2)}) copy-start(bf16[2,2,128,896]{3,2,1,0:T(8,128)(2,1)} %copy-done.1) | copy-start | bytes 2752516
  114.9 24.1 %collective-permute-start.9 = (bf16[2,112,1024]{2,1,0:T(8,128)(2,1)}, bf16[2,112,1024]{2,1,0:T(8,128)(2,1)}, u32[]{:S(2)}, u32[]{:S(2)}) collective-permute-start(bf16[2,112,1024]{2,1,0:T(8,128)(2,1)} %get-tuple-element.25), channel_id=1, source_target_pairs={{0,384},{64,448},{128,0},{192,64},{256,128},{320,192},{384,256},{4... | collective-permute-start | bytes 1376264 | tf_op jit(solution)/shard_map/ppermute | solution.py:46
  119.8 24.5 %collective-permute-start.8 = (bf16[2,112,1024]{2,1,0:T(8,128)(2,1)}, bf16[2,112,1024]{2,1,0:T(8,128)(2,1)}, u32[]{:S(2)}, u32[]{:S(2)}) collective-permute-start(bf16[2,112,1024]{2,1,0:T(8,128)(2,1)} %get-tuple-element.24), channel_id=1, source_target_pairs={{0,128},{64,192},{128,256},{192,320},{256,384},{320,448},{384,0},{... | collective-permute-start | bytes 1376264 | tf_op jit(solution)/shard_map/ppermute | solution.py:46
  121.7 22.6 %collective-permute-start.7 = (bf16[2,112,1024]{2,1,0:T(8,128)(2,1)}, bf16[2,112,1024]{2,1,0:T(8,128)(2,1)}, u32[]{:S(2)}, u32[]{:S(2)}) collective-permute-start(bf16[2,112,1024]{2,1,0:T(8,128)(2,1)} %get-tuple-element.23), channel_id=1, source_target_pairs={{0,256},{64,320},{128,384},{192,448},{256,0},{320,64},{384,128},{4... | collective-permute-start | bytes 1376264 | tf_op jit(solution)/shard_map/ppermute | solution.py:46
  128.0 22.6 %collective-permute-start.5 = (bf16[2,128,896]{2,1,0:T(8,128)(2,1)}, bf16[2,128,896]{2,1,0:T(8,128)(2,1)}, u32[]{:S(2)}, u32[]{:S(2)}) collective-permute-start(bf16[2,128,896]{2,1,0:T(8,128)(2,1)} %get-tuple-element.20), channel_id=1, source_target_pairs={{0,1},{1,0},{2,3},{3,2},{4,5},{5,4},{6,7},{7,6},{8,9},{9,8},{10,11... | collective-permute-start | bytes 1376264 | tf_op jit(solution)/shard_map/ppermute | solution.py:60
  146.1 14.3 %copy-start.3 = (bf16[128,896]{1,0:T(8,128)(2,1)S(1)}, bf16[128,896]{1,0:T(8,128)(2,1)}, u32[]{:S(2)}) copy-start(bf16[128,896]{1,0:T(8,128)(2,1)} %param.5) | copy-start | bytes 688132
  146.1 14.3 %copy-start.4 = (bf16[128,896]{1,0:T(8,128)(2,1)S(1)}, bf16[128,896]{1,0:T(8,128)(2,1)}, u32[]{:S(2)}) copy-start(bf16[128,896]{1,0:T(8,128)(2,1)} %param.4) | copy-start | bytes 688132
  146.1 11.7 %collective-permute-start.10 = (bf16[112,1024]{1,0:T(8,128)(2,1)S(1)}, bf16[112,1024]{1,0:T(8,128)(2,1)S(1)}, u32[]{:S(2)}, u32[]{:S(2)}) collective-permute-start(bf16[112,1024]{1,0:T(8,128)(2,1)S(1)} %fusion.9), channel_id=1, source_target_pairs={{0,64},{64,0},{128,192},{192,128},{256,320},{320,256},{384,448},{4... | collective-permute-start | bytes 688136 | tf_op jit(solution)/shard_map/ppermute | solution.py:49
  151.8 8.6 %collective-permute-start.6 = (bf16[128,896]{1,0:T(8,128)(2,1)S(1)}, bf16[128,896]{1,0:T(8,128)(2,1)S(1)}, u32[]{:S(2)}, u32[]{:S(2)}) collective-permute-start(bf16[128,896]{1,0:T(8,128)(2,1)S(1)} %fusion.8), channel_id=1, source_target_pairs={{0,2},{1,3},{2,0},{3,1},{4,6},{5,7},{6,4},{7,5},{8,10},{9,11},{10,... | collective-permute-start | bytes 688136 | tf_op jit(solution)/shard_map/ppermute | solution.py:63

commit v2 on v1

--- a/solution.py
+++ b/solution.py
@@ -20,11 +20,19 @@
     return lax.all_gather(block, "row", axis=0, tiled=False, axis_index_groups=groups)
 
 
+def two_away(array):
+    rows, cols = lax.axis_size("row"), lax.axis_size("col")
+    route = [
+        (r * cols + c, (r + (2 if c % 2 == 0 else -2)) % rows * cols + c) for r in range(rows) for c in range(cols)
+    ]
+    return lax.ppermute(array, ("row", "col"), route)
+
+
 def gather_near(same):
     low = lax.axis_index("row") & 3
     sets = [same]
     for by in (1, 2, 15):
-        sets.append(shifted(same, "row", by))
+        sets.append(two_away(same) if by == 2 else shifted(same, "row", by))
     whole = [lax.select_n((low - k) & 3, *sets) for k in range(4)]
     return jnp.stack(whole, axis=1).reshape(-1, same.shape[-1])
 

time: 163 us -> 159 us (0.975)
  the two profiles are of different devices: /device:TPU:2 before, /device:TPU:34 now
where the time goes in v2:
time: 159 us; the launch traced here: 158 us
  waiting for transfers between devices  71 us (45%)
  starting transfers between devices  43.9 us (28%)
  blocking collectives  25.9 us (16%)
  other arithmetic  9.43 us (6%)
  matrix products  4.71 us (3%)
  local copies, waits for them, and re-layouts  2.24 us (1%)
    ppermute x1, waiting for transfers between devices, two_away(): return lax.ppermute(array, ('row', 'col'), route)  45.9 us
    all_gather x1, blocking collectives, gather_apart(): lax.all_gather(block, 'row', axis=0, tiled=False, axis_index_groups=groups)  25.9 us
    ppermute x3, waiting for transfers between devices, sum_over_dp(): got = lax.ppermute(mine, 'dp', [(i, (i + 2 * dy) % 8) for i in range(8)])  16.1 us
    ppermute x3, starting transfers between devices, sum_over_dp(): got = lax.ppermute(mine, 'dp', [(i, (i + 2 * dy) % 8) for i in range(8)])  10.9 us
    all_to_all x1, starting transfers between devices, sum_over_row(): parts = lax.all_to_all(parts, 'row', 0, 0, tiled=True)  7.59 us
    ppermute x2, starting transfers between devices, shifted(): lax.ppermute(array, axis, [(i, (i + by) % count) for i in range(count)])  6.5 us
    ppermute x1, starting transfers between devices, sum_over_dp(): away = lax.ppermute(away, 'dp', [(i, i ^ 1) for i in range(8)])  4.46 us
    ppermute x1, starting transfers between devices, two_away(): return lax.ppermute(array, ('row', 'col'), route)  4.26 us
  transfers between devices with their start and end apart: 12, of which 8 were waited for; matrix products, arithmetic and copies ran while one was open for 7% of the time, Pallas kernels for 0%

profile of v2, /device:TPU:34, one launch (start us, length us, event | category | flops | bytes accessed | tf_op | source)
XLA Modules:
  0.0 158.1 jit_solution(18120056301389228951)
XLA Ops:
  0.6 1.3 fusion
  2.0 2.4 %collective-permute-start = (bf16[128,896]{1,0:T(8,128)(2,1)S(1)}, bf16[128,896]{1,0:T(8,128)(2,1)S(1)}, u32[]{:S(2)}, u32[]{:S(2)}) collective-permute-start(bf16[128,896]{1,0:T(8,128)(2,1)S(1)} %fusion), channel_id=1, source_target_pairs={{0,2},{1,3},{2,0},{3,1},{4,6},{5,7},{6,4},{7,5},{8,10},{9,11},{10,... | collective-permute-start | bytes 688136 | tf_op jit(solution)/shard_map/ppermute | solution.py:82
  4.4 25.9 %all-gather = bf16[128,1024]{1,0:T(8,128)(2,1)S(1)} all-gather(bf16[32,1024]{1,0:T(8,128)(2,1)} %param.6), channel_id=2, replica_groups={{0,16,32,48},{4,20,36,52},{8,24,40,56},{12,28,44,60},{1,17,33,49},{5,21..., dimensions={0}, use_global_device_ids=true | all-gather | bytes 327680 | tf_op jit(solution)/shard_map/all_gather | solution.py:20
  30.5 1.9 %collective-permute-start.1 = (bf16[2,128,896]{2,1,0:T(8,128)(2,1)S(1)}, bf16[2,128,896]{2,1,0:T(8,128)(2,1)}, u32[]{:S(2)}, u32[]{:S(2)}) collective-permute-start(bf16[2,128,896]{2,1,0:T(8,128)(2,1)S(1)} %pad_maximum_fusion.2), channel_id=1, source_target_pairs={{0,1},{1,0},{2,3},{3,2},{4,5},{5,4},{6,7},{7,6},{8,9},{9,8},{10,11... | collective-permute-start | bytes 1376264 | tf_op jit(solution)/shard_map/ppermute | solution.py:87
  32.4 1.9 %collective-permute-done.1 = bf16[2,128,896]{2,1,0:T(8,128)(2,1)} collective-permute-done((bf16[2,128,896]{2,1,0:T(8,128)(2,1)S(1)}, bf16[2,128,896]{2,1,0:T(8,128)(2,1)}, u32[]{:S(2)}, u32[]{:S(2)}) %collective-permute-start.1) | collective-permute-done | bytes 458784 | tf_op jit(solution)/shard_map/ppermute | solution.py:87
  35.5 2.3 %convolution_convert_fusion = bf16[512,1024]{1,0:T(8,128)(2,1)} fusion(bf16[512,896]{1,0:T(8,128)(2,1)S(1)} %bitcast.68, bf16[896,1024]{1,0:T(8,128)(2,1)S(1)} %copy-done), kind=kOutput, calls=%fused_computation.1 | convolution fusion | flops 940048384 | bytes 3801088 | tf_op jit(solution)/shard_map/dot_general | solution.py:90
  37.8 7.6 %all-to-all-start = ((bf16[16,32,1024]{2,1,0:T(8,128)(2,1)}), bf16[16,32,1024]{2,1,0:T(8,128)(2,1)S(1)}, u32[]{:S(2)}, u32[]{:S(2)}) async-start(bf16[16,32,1024]{2,1,0:T(8,128)(2,1)} %bitcast.65), calls=%async_computation | async-start | bytes 2097152 | tf_op jit(solution)/shard_map/all_to_all | solution.py:43
  45.4 4.3 %collective-permute-start.3 = (bf16[4,32,1024]{2,1,0:T(8,128)(2,1)S(1)}, bf16[4,32,1024]{2,1,0:T(8,128)(2,1)S(1)}, u32[]{:S(2)}, u32[]{:S(2)}) collective-permute-start(bf16[4,32,1024]{2,1,0:T(8,128)(2,1)S(1)} %bitcast.61), channel_id=1, source_target_pairs={{0,8},{1,57},{2,10},{3,59},{4,12},{5,61},{6,14},{7,63},{8,16},{9,1... | collective-permute-start | bytes 786440 | tf_op jit(solution)/shard_map/ppermute | solution.py:28
  49.7 2.5 %collective-permute-start.4 = (bf16[4,32,1024]{2,1,0:T(8,128)(2,1)S(1)}, bf16[4,32,1024]{2,1,0:T(8,128)(2,1)}, u32[]{:S(2)}, u32[]{:S(2)}) collective-permute-start(bf16[4,32,1024]{2,1,0:T(8,128)(2,1)S(1)} %bitcast.62), channel_id=1, source_target_pairs={{0,60},{4,0},{8,4},{12,8},{16,12},{20,16},{24,20},{28,24},{32,28},... | collective-permute-start | bytes 786440 | tf_op jit(solution)/shard_map/ppermute | solution.py:11
  52.2 4.0 %collective-permute-start.2 = (bf16[4,32,1024]{2,1,0:T(8,128)(2,1)S(1)}, bf16[4,32,1024]{2,1,0:T(8,128)(2,1)}, u32[]{:S(2)}, u32[]{:S(2)}) collective-permute-start(bf16[4,32,1024]{2,1,0:T(8,128)(2,1)S(1)} %bitcast.63), channel_id=1, source_target_pairs={{0,4},{4,8},{8,12},{12,16},{16,20},{20,24},{24,28},{28,32},{32,36}... | collective-permute-start | bytes 786440 | tf_op jit(solution)/shard_map/ppermute | solution.py:11
  56.2 45.9 %collective-permute-done.3 = bf16[4,32,1024]{2,1,0:T(8,128)(2,1)S(1)} collective-permute-done((bf16[4,32,1024]{2,1,0:T(8,128)(2,1)S(1)}, bf16[4,32,1024]{2,1,0:T(8,128)(2,1)S(1)}, u32[]{:S(2)}, u32[]{:S(2)}) %collective-permute-start.3) | collective-permute-done | bytes 262176 | tf_op jit(solution)/shard_map/ppermute | solution.py:28
  105.3 1.3 dynamic-slice_bitcast_fusion
  106.6 4.9 %collective-permute-start.9 = (bf16[2,112,1024]{2,1,0:T(8,128)(2,1)}, bf16[2,112,1024]{2,1,0:T(8,128)(2,1)}, u32[]{:S(2)}, u32[]{:S(2)}) collective-permute-start(bf16[2,112,1024]{2,1,0:T(8,128)(2,1)} %get-tuple-element.25), channel_id=1, source_target_pairs={{0,384},{64,448},{128,0},{192,64},{256,128},{320,192},{384,256},{4... | collective-permute-start | bytes 1376264 | tf_op jit(solution)/shard_map/ppermute | solution.py:54
  111.5 1.9 %collective-permute-start.8 = (bf16[2,112,1024]{2,1,0:T(8,128)(2,1)}, bf16[2,112,1024]{2,1,0:T(8,128)(2,1)}, u32[]{:S(2)}, u32[]{:S(2)}) collective-permute-start(bf16[2,112,1024]{2,1,0:T(8,128)(2,1)} %get-tuple-element.24), channel_id=1, source_target_pairs={{0,128},{64,192},{128,256},{192,320},{256,384},{320,448},{384,0},{... | collective-permute-start | bytes 1376264 | tf_op jit(solution)/shard_map/ppermute | solution.py:54
  113.4 4.1 %collective-permute-start.7 = (bf16[2,112,1024]{2,1,0:T(8,128)(2,1)}, bf16[2,112,1024]{2,1,0:T(8,128)(2,1)}, u32[]{:S(2)}, u32[]{:S(2)}) collective-permute-start(bf16[2,112,1024]{2,1,0:T(8,128)(2,1)} %get-tuple-element.23), channel_id=1, source_target_pairs={{0,256},{64,320},{128,384},{192,448},{256,0},{320,64},{384,128},{4... | collective-permute-start | bytes 1376264 | tf_op jit(solution)/shard_map/ppermute | solution.py:54
  117.5 1.3 convolution_convert_fusion.1
  119.7 2.1 %collective-permute-start.5 = (bf16[2,128,896]{2,1,0:T(8,128)(2,1)}, bf16[2,128,896]{2,1,0:T(8,128)(2,1)}, u32[]{:S(2)}, u32[]{:S(2)}) collective-permute-start(bf16[2,128,896]{2,1,0:T(8,128)(2,1)} %get-tuple-element.20), channel_id=1, source_target_pairs={{0,1},{1,0},{2,3},{3,2},{4,5},{5,4},{6,7},{7,6},{8,9},{9,8},{10,11... | collective-permute-start | bytes 1376264 | tf_op jit(solution)/shard_map/ppermute | solution.py:68
  121.7 10.7 %collective-permute-done.9 = bf16[2,112,1024]{2,1,0:T(8,128)(2,1)} collective-permute-done((bf16[2,112,1024]{2,1,0:T(8,128)(2,1)}, bf16[2,112,1024]{2,1,0:T(8,128)(2,1)}, u32[]{:S(2)}, u32[]{:S(2)}) %collective-permute-start.9) | collective-permute-done | bytes 458784 | tf_op jit(solution)/shard_map/ppermute | solution.py:54
  132.5 5.4 %collective-permute-done.8 = bf16[2,112,1024]{2,1,0:T(8,128)(2,1)} collective-permute-done((bf16[2,112,1024]{2,1,0:T(8,128)(2,1)}, bf16[2,112,1024]{2,1,0:T(8,128)(2,1)}, u32[]{:S(2)}, u32[]{:S(2)}) %collective-permute-start.8) | collective-permute-done | bytes 458784 | tf_op jit(solution)/shard_map/ppermute | solution.py:54
  137.9 1.7 %convert_add_fusion = f32[2,112,1024]{2,1,0:T(8,128)S(1)} fusion(bf16[2,112,1024]{2,1,0:T(8,128)(2,1)} %collective-permute-done.9, bf16[2,112,1024]{2,1,0:T(8,128)(2,1)} %collective-permute-done.8, bf16[2,112,1024]{2,1,0:T(8,128)(2,1)} %collective-permute-done.7, bf16[2,112,1024]{2,1,0:T(8,128)(2,1)} %get-tuple-element.22), kind=kLoop, calls=%fused_computation.5 | loop fusion | flops 1605632 | bytes 2752512 | tf_op jit(solution)/shard_map/add | solution.py:55
  139.7 4.5 %collective-permute-start.10 = (bf16[112,1024]{1,0:T(8,128)(2,1)S(1)}, bf16[112,1024]{1,0:T(8,128)(2,1)S(1)}, u32[]{:S(2)}, u32[]{:S(2)}) collective-permute-start(bf16[112,1024]{1,0:T(8,128)(2,1)S(1)} %fusion.9), channel_id=1, source_target_pairs={{0,64},{64,0},{128,192},{192,128},{256,320},{320,256},{384,448},{4... | collective-permute-start | bytes 688136 | tf_op jit(solution)/shard_map/ppermute | solution.py:57
  145.3 3.7 %collective-permute-start.6 = (bf16[128,896]{1,0:T(8,128)(2,1)S(1)}, bf16[128,896]{1,0:T(8,128)(2,1)S(1)}, u32[]{:S(2)}, u32[]{:S(2)}) collective-permute-start(bf16[128,896]{1,0:T(8,128)(2,1)S(1)} %fusion.8), channel_id=1, source_target_pairs={{0,2},{1,3},{2,0},{3,1},{4,6},{5,7},{6,4},{7,5},{8,10},{9,11},{10,... | collective-permute-start | bytes 688136 | tf_op jit(solution)/shard_map/ppermute | solution.py:71
  149.0 2.6 %collective-permute-done.10 = bf16[112,1024]{1,0:T(8,128)(2,1)S(1)} collective-permute-done((bf16[112,1024]{1,0:T(8,128)(2,1)S(1)}, bf16[112,1024]{1,0:T(8,128)(2,1)S(1)}, u32[]{:S(2)}, u32[]{:S(2)}) %collective-permute-start.10) | collective-permute-done | bytes 229408 | tf_op jit(solution)/shard_map/ppermute | solution.py:57
  152.5 3.7 %collective-permute-done.6 = bf16[128,896]{1,0:T(8,128)(2,1)S(1)} collective-permute-done((bf16[128,896]{1,0:T(8,128)(2,1)S(1)}, bf16[128,896]{1,0:T(8,128)(2,1)S(1)}, u32[]{:S(2)}, u32[]{:S(2)}) %collective-permute-start.6) | collective-permute-done | bytes 229408 | tf_op jit(solution)/shard_map/ppermute | solution.py:71
  (30 shorter events, 9.2 us)
Async XLA Ops:
  0.6 34.9 %copy-start = (bf16[896,1024]{1,0:T(8,128)(2,1)S(1)}, bf16[896,1024]{1,0:T(8,128)(2,1)}, u32[]{:S(2)}) copy-start(bf16[896,1024]{1,0:T(8,128)(2,1)} %param.7) | copy-start | bytes 5505028
  2.0 28.4 %collective-permute-start = (bf16[128,896]{1,0:T(8,128)(2,1)S(1)}, bf16[128,896]{1,0:T(8,128)(2,1)S(1)}, u32[]{:S(2)}, u32[]{:S(2)}) collective-permute-start(bf16[128,896]{1,0:T(8,128)(2,1)S(1)} %fusion), channel_id=1, source_target_pairs={{0,2},{1,3},{2,0},{3,1},{4,6},{5,7},{6,4},{7,5},{8,10},{9,11},{10,... | collective-permute-start | bytes 688136 | tf_op jit(solution)/shard_map/ppermute | solution.py:82
  30.5 3.8 %collective-permute-start.1 = (bf16[2,128,896]{2,1,0:T(8,128)(2,1)S(1)}, bf16[2,128,896]{2,1,0:T(8,128)(2,1)}, u32[]{:S(2)}, u32[]{:S(2)}) collective-permute-start(bf16[2,128,896]{2,1,0:T(8,128)(2,1)S(1)} %pad_maximum_fusion.2), channel_id=1, source_target_pairs={{0,1},{1,0},{2,3},{3,2},{4,5},{5,4},{6,7},{7,6},{8,9},{9,8},{10,11... | collective-permute-start | bytes 1376264 | tf_op jit(solution)/shard_map/ppermute | solution.py:87
  35.5 2.3 %copy-start.1 = (bf16[2,2,128,896]{3,2,1,0:T(8,128)(2,1)}, bf16[2,2,128,896]{3,2,1,0:T(8,128)(2,1)S(1)}, u32[]{:S(2)}) copy-start(bf16[2,2,128,896]{3,2,1,0:T(8,128)(2,1)S(1)} %pad_maximum_fusion.1) | copy-start | bytes 2752516
  37.8 119.4 %all-to-all-start = ((bf16[16,32,1024]{2,1,0:T(8,128)(2,1)}), bf16[16,32,1024]{2,1,0:T(8,128)(2,1)S(1)}, u32[]{:S(2)}, u32[]{:S(2)}) async-start(bf16[16,32,1024]{2,1,0:T(8,128)(2,1)} %bitcast.65), calls=%async_computation | async-start | bytes 2097152 | tf_op jit(solution)/shard_map/all_to_all | solution.py:43
  45.4 56.7 %collective-permute-start.3 = (bf16[4,32,1024]{2,1,0:T(8,128)(2,1)S(1)}, bf16[4,32,1024]{2,1,0:T(8,128)(2,1)S(1)}, u32[]{:S(2)}, u32[]{:S(2)}) collective-permute-start(bf16[4,32,1024]{2,1,0:T(8,128)(2,1)S(1)} %bitcast.61), channel_id=1, source_target_pairs={{0,8},{1,57},{2,10},{3,59},{4,12},{5,61},{6,14},{7,63},{8,16},{9,1... | collective-permute-start | bytes 786440 | tf_op jit(solution)/shard_map/ppermute | solution.py:28
  49.7 52.5 %collective-permute-start.4 = (bf16[4,32,1024]{2,1,0:T(8,128)(2,1)S(1)}, bf16[4,32,1024]{2,1,0:T(8,128)(2,1)}, u32[]{:S(2)}, u32[]{:S(2)}) collective-permute-start(bf16[4,32,1024]{2,1,0:T(8,128)(2,1)S(1)} %bitcast.62), channel_id=1, source_target_pairs={{0,60},{4,0},{8,4},{12,8},{16,12},{20,16},{24,20},{28,24},{32,28},... | collective-permute-start | bytes 786440 | tf_op jit(solution)/shard_map/ppermute | solution.py:11
  52.2 50.7 %collective-permute-start.2 = (bf16[4,32,1024]{2,1,0:T(8,128)(2,1)S(1)}, bf16[4,32,1024]{2,1,0:T(8,128)(2,1)}, u32[]{:S(2)}, u32[]{:S(2)}) collective-permute-start(bf16[4,32,1024]{2,1,0:T(8,128)(2,1)S(1)} %bitcast.63), channel_id=1, source_target_pairs={{0,4},{4,8},{8,12},{12,16},{16,20},{20,24},{24,28},{28,32},{32,36}... | collective-permute-start | bytes 786440 | tf_op jit(solution)/shard_map/ppermute | solution.py:11
  56.2 47.9 %copy-start.2 = (bf16[2,2,128,896]{3,2,1,0:T(8,128)(2,1)S(1)}, bf16[2,2,128,896]{3,2,1,0:T(8,128)(2,1)}, u32[]{:S(2)}) copy-start(bf16[2,2,128,896]{3,2,1,0:T(8,128)(2,1)} %copy-done.1) | copy-start | bytes 2752516
  106.6 25.9 %collective-permute-start.9 = (bf16[2,112,1024]{2,1,0:T(8,128)(2,1)}, bf16[2,112,1024]{2,1,0:T(8,128)(2,1)}, u32[]{:S(2)}, u32[]{:S(2)}) collective-permute-start(bf16[2,112,1024]{2,1,0:T(8,128)(2,1)} %get-tuple-element.25), channel_id=1, source_target_pairs={{0,384},{64,448},{128,0},{192,64},{256,128},{320,192},{384,256},{4... | collective-permute-start | bytes 1376264 | tf_op jit(solution)/shard_map/ppermute | solution.py:54
  111.5 26.4 %collective-permute-start.8 = (bf16[2,112,1024]{2,1,0:T(8,128)(2,1)}, bf16[2,112,1024]{2,1,0:T(8,128)(2,1)}, u32[]{:S(2)}, u32[]{:S(2)}) collective-permute-start(bf16[2,112,1024]{2,1,0:T(8,128)(2,1)} %get-tuple-element.24), channel_id=1, source_target_pairs={{0,128},{64,192},{128,256},{192,320},{256,384},{320,448},{384,0},{... | collective-permute-start | bytes 1376264 | tf_op jit(solution)/shard_map/ppermute | solution.py:54
  113.4 24.5 %collective-permute-start.7 = (bf16[2,112,1024]{2,1,0:T(8,128)(2,1)}, bf16[2,112,1024]{2,1,0:T(8,128)(2,1)}, u32[]{:S(2)}, u32[]{:S(2)}) collective-permute-start(bf16[2,112,1024]{2,1,0:T(8,128)(2,1)} %get-tuple-element.23), channel_id=1, source_target_pairs={{0,256},{64,320},{128,384},{192,448},{256,0},{320,64},{384,128},{4... | collective-permute-start | bytes 1376264 | tf_op jit(solution)/shard_map/ppermute | solution.py:54
  119.7 24.5 %collective-permute-start.5 = (bf16[2,128,896]{2,1,0:T(8,128)(2,1)}, bf16[2,128,896]{2,1,0:T(8,128)(2,1)}, u32[]{:S(2)}, u32[]{:S(2)}) collective-permute-start(bf16[2,128,896]{2,1,0:T(8,128)(2,1)} %get-tuple-element.20), channel_id=1, source_target_pairs={{0,1},{1,0},{2,3},{3,2},{4,5},{5,4},{6,7},{7,6},{8,9},{9,8},{10,11... | collective-permute-start | bytes 1376264 | tf_op jit(solution)/shard_map/ppermute | solution.py:68
  139.7 16.5 %copy-start.3 = (bf16[128,896]{1,0:T(8,128)(2,1)S(1)}, bf16[128,896]{1,0:T(8,128)(2,1)}, u32[]{:S(2)}) copy-start(bf16[128,896]{1,0:T(8,128)(2,1)} %param.5) | copy-start | bytes 688132
  139.7 16.5 %copy-start.4 = (bf16[128,896]{1,0:T(8,128)(2,1)S(1)}, bf16[128,896]{1,0:T(8,128)(2,1)}, u32[]{:S(2)}) copy-start(bf16[128,896]{1,0:T(8,128)(2,1)} %param.4) | copy-start | bytes 688132
  139.7 12.0 %collective-permute-start.10 = (bf16[112,1024]{1,0:T(8,128)(2,1)S(1)}, bf16[112,1024]{1,0:T(8,128)(2,1)S(1)}, u32[]{:S(2)}, u32[]{:S(2)}) collective-permute-start(bf16[112,1024]{1,0:T(8,128)(2,1)S(1)} %fusion.9), channel_id=1, source_target_pairs={{0,64},{64,0},{128,192},{192,128},{256,320},{320,256},{384,448},{4... | collective-permute-start | bytes 688136 | tf_op jit(solution)/shard_map/ppermute | solution.py:57
  145.3 10.9 %collective-permute-start.6 = (bf16[128,896]{1,0:T(8,128)(2,1)S(1)}, bf16[128,896]{1,0:T(8,128)(2,1)S(1)}, u32[]{:S(2)}, u32[]{:S(2)}) collective-permute-start(bf16[128,896]{1,0:T(8,128)(2,1)S(1)} %fusion.8), channel_id=1, source_target_pairs={{0,2},{1,3},{2,0},{3,1},{4,6},{5,7},{6,4},{7,5},{8,10},{9,11},{10,... | collective-permute-start | bytes 688136 | tf_op jit(solution)/shard_map/ppermute | solution.py:71

commit v3 on v2

--- a/solution.py
+++ b/solution.py
@@ -29,18 +29,31 @@
 
 
 def gather_near(same):
-    low = lax.axis_index("row") & 3
     sets = [same]
     for by in (1, 2, 15):
         sets.append(two_away(same) if by == 2 else shifted(same, "row", by))
+    return sets
+
+
+def assemble(sets, low):
+    same = sets[0]
     whole = [lax.select_n((low - k) & 3, *sets) for k in range(4)]
     return jnp.stack(whole, axis=1).reshape(-1, same.shape[-1])
 
 
+def pair_rows(parts):
+    parts = parts.reshape((8, 2, parts.shape[0] // 16) + parts.shape[1:])
+    parity = lax.axis_index("row") & 1
+    other = lax.dynamic_index_in_dim(parts, 1 - parity, 1, keepdims=False)
+    mine = lax.dynamic_index_in_dim(parts, parity, 1, keepdims=False)
+    other, mine = hold((other, mine))
+    other = lax.ppermute(other, "row", [(i, i ^ 1) for i in range(lax.axis_size("row"))])
+    return (mine.astype(jnp.float32) + other.astype(jnp.float32)).astype(jnp.bfloat16)
+
+
 def sum_over_row(parts):
-    count = lax.axis_size("row")
-    parts = parts.reshape((count, parts.shape[0] // count) + parts.shape[1:])
-    parts = lax.all_to_all(parts, "row", 0, 0, tiled=True)
+    groups = [list(range(0, 16, 2)), list(range(1, 16, 2))]
+    parts = lax.all_to_all(parts, "row", 0, 0, tiled=True, axis_index_groups=groups)
     return jnp.sum(parts.astype(jnp.float32), axis=0)
 
 
@@ -81,14 +94,16 @@
     me = lax.axis_index("col")
     ahead = lax.ppermute(hidden, "col", [(i, i ^ 2) for i in range(4)])
     grad_apart = gather_apart(out_grad)
-    grad_all = gather_near(grad_apart)
+    sets = gather_near(grad_apart)
     ahead, grad_late = hold((ahead, grad_apart))
     pair = jnp.stack([lax.select_n(me >> 1, hidden, ahead), lax.select_n(me >> 1, ahead, hidden)])
     beside = lax.ppermute(pair, "col", [(i, i ^ 1) for i in range(4)])
     hidden_all = jnp.stack([lax.select_n(me & 1, pair, beside), lax.select_n(me & 1, beside, pair)], axis=1)
     hidden_all = hidden_all.reshape(-1, hidden.shape[1])
     layer_parts = jnp.dot(hidden_all, down_weight, preferred_element_type=jnp.float32).astype(jnp.bfloat16)
-    layer_out = sum_over_row(layer_parts).astype(jnp.bfloat16)
+    layer_parts, low = hold((layer_parts, lax.axis_index("row") & 3))
+    grad_all = assemble(sets, low)
+    layer_out = sum_over_row(pair_rows(layer_parts)).astype(jnp.bfloat16)
 
     hidden_all, grad_all = hold((hidden_all, grad_all))
     factor = 1.0 / (hidden_all.shape[0] * lax.axis_size("dp")) ** 0.5

time: 159 us -> 120 us (0.75)
  the two profiles are of different devices: /device:TPU:34 before, /device:TPU:32 now
where the time goes in v3:
time: 120 us
  starting transfers between devices  44.2 us (37%)
  waiting for transfers between devices  29.6 us (25%)
  blocking collectives  25.9 us (22%)
  other arithmetic  9.23 us (8%)
  matrix products  4.98 us (4%)
  local copies, waits for them, and re-layouts  4.65 us (4%)
    all_gather x1, blocking collectives, gather_apart(): lax.all_gather(block, 'row', axis=0, tiled=False, axis_index_groups=groups)  25.9 us
    ppermute x3, waiting for transfers between devices, sum_over_dp(): got = lax.ppermute(mine, 'dp', [(i, (i + 2 * dy) % 8) for i in range(8)])  14.4 us
    ppermute x3, starting transfers between devices, sum_over_dp(): got = lax.ppermute(mine, 'dp', [(i, (i + 2 * dy) % 8) for i in range(8)])  10.9 us
    ppermute x1, waiting for transfers between devices, pair_rows(): lax.ppermute(other, 'row', [(i, i ^ 1) for i in range(lax.axis_size('row'...  6.67 us
    all_to_all x1, starting transfers between devices, sum_over_row(): lax.all_to_all(parts, 'row', 0, 0, tiled=True, axis_index_groups=groups)  6.65 us
    ppermute x2, starting transfers between devices, shifted(): lax.ppermute(array, axis, [(i, (i + by) % count) for i in range(count)])  5.84 us
    ppermute x1, starting transfers between devices, sum_over_dp(): away = lax.ppermute(away, 'dp', [(i, i ^ 1) for i in range(8)])  4.77 us
    ppermute x1, waiting for transfers between devices, sum_over_dp(): away = lax.ppermute(away, 'dp', [(i, i ^ 1) for i in range(8)])  3.9 us
  transfers between devices with their start and end apart: 13, of which 6 were waited for; matrix products, arithmetic and copies ran while one was open for 12% of the time, Pallas kernels for 0%

profile of v3, /device:TPU:32, one launch (start us, length us, event | category | flops | bytes accessed | tf_op | source)
XLA Modules:
  0.0 119.5 jit_solution(486380356090022916)
XLA Ops:
  0.6 1.3 %fusion = bf16[128,896]{1,0:T(8,128)(2,1)S(1)} fusion(bf16[128,896]{1,0:T(8,128)(2,1)} %param.5, bf16[128,896]{1,0:T(8,128)(2,1)} %param.4), kind=kLoop, calls=%fused_computation.15 | loop fusion | flops 917504 | bytes 688128 | tf_op jit(solution)/shard_map/convert_element_type | solution.py:93
  2.0 3.4 %collective-permute-start = (bf16[128,896]{1,0:T(8,128)(2,1)S(1)}, bf16[128,896]{1,0:T(8,128)(2,1)S(1)}, u32[]{:S(2)}, u32[]{:S(2)}) collective-permute-start(bf16[128,896]{1,0:T(8,128)(2,1)S(1)} %fusion), channel_id=1, source_target_pairs={{0,2},{1,3},{2,0},{3,1},{4,6},{5,7},{6,4},{7,5},{8,10},{9,11},{10,... | collective-permute-start | bytes 688136 | tf_op jit(solution)/shard_map/ppermute | solution.py:95
  5.4 25.9 %all-gather = bf16[128,1024]{1,0:T(8,128)(2,1)S(1)} all-gather(bf16[32,1024]{1,0:T(8,128)(2,1)} %param.6), channel_id=2, replica_groups={{0,16,32,48},{4,20,36,52},{8,24,40,56},{12,28,44,60},{1,17,33,49},{5,21..., dimensions={0}, use_global_device_ids=true | all-gather | bytes 327680 | tf_op jit(solution)/shard_map/all_gather | solution.py:20
  31.4 1.9 %collective-permute-start.1 = (bf16[2,128,896]{2,1,0:T(8,128)(2,1)S(1)}, bf16[2,128,896]{2,1,0:T(8,128)(2,1)S(1)}, u32[]{:S(2)}, u32[]{:S(2)}) collective-permute-start(bf16[2,128,896]{2,1,0:T(8,128)(2,1)S(1)} %pad_maximum_fusion.2), channel_id=1, source_target_pairs={{0,1},{1,0},{2,3},{3,2},{4,5},{5,4},{6,7},{7,6},{8,9},{9,8},{10,11... | collective-permute-start | bytes 1376264 | tf_op jit(solution)/shard_map/ppermute | solution.py:100
  33.3 3.3 %collective-permute-start.4 = (bf16[4,32,1024]{2,1,0:T(8,128)(2,1)S(1)}, bf16[4,32,1024]{2,1,0:T(8,128)(2,1)}, u32[]{:S(2)}, u32[]{:S(2)}) collective-permute-start(bf16[4,32,1024]{2,1,0:T(8,128)(2,1)S(1)} %bitcast.65), channel_id=1, source_target_pairs={{0,8},{1,57},{2,10},{3,59},{4,12},{5,61},{6,14},{7,63},{8,16},{9,1... | collective-permute-start | bytes 786440 | tf_op jit(solution)/shard_map/ppermute | solution.py:28
  36.6 3.0 %collective-permute-start.5 = (bf16[4,32,1024]{2,1,0:T(8,128)(2,1)S(1)}, bf16[4,32,1024]{2,1,0:T(8,128)(2,1)}, u32[]{:S(2)}, u32[]{:S(2)}) collective-permute-start(bf16[4,32,1024]{2,1,0:T(8,128)(2,1)S(1)} %bitcast.66), channel_id=1, source_target_pairs={{0,60},{4,0},{8,4},{12,8},{16,12},{20,16},{24,20},{28,24},{32,28},... | collective-permute-start | bytes 786440 | tf_op jit(solution)/shard_map/ppermute | solution.py:11
  39.7 2.8 %collective-permute-start.3 = (bf16[4,32,1024]{2,1,0:T(8,128)(2,1)S(1)}, bf16[4,32,1024]{2,1,0:T(8,128)(2,1)}, u32[]{:S(2)}, u32[]{:S(2)}) collective-permute-start(bf16[4,32,1024]{2,1,0:T(8,128)(2,1)S(1)} %bitcast.67), channel_id=1, source_target_pairs={{0,4},{4,8},{8,12},{12,16},{16,20},{20,24},{24,28},{28,32},{32,36}... | collective-permute-start | bytes 786440 | tf_op jit(solution)/shard_map/ppermute | solution.py:11
  45.1 3.3 %collective-permute-start.2 = (bf16[8,32,1024]{2,1,0:T(8,128)(2,1)S(1)}, bf16[8,32,1024]{2,1,0:T(8,128)(2,1)S(1)}, u32[]{:S(2)}, u32[]{:S(2)}) collective-permute-start(bf16[8,32,1024]{2,1,0:T(8,128)(2,1)S(1)} %get-tuple-element.22), channel_id=1, source_target_pairs={{0,4},{4,0},{8,12},{12,8},{16,20},{20,16},{24,28},{28,24},{32,36},... | collective-permute-start | bytes 1572872 | tf_op jit(solution)/shard_map/ppermute | solution.py:50
  48.5 3.5 %collective-permute-done.3 = bf16[4,32,1024]{2,1,0:T(8,128)(2,1)} collective-permute-done((bf16[4,32,1024]{2,1,0:T(8,128)(2,1)S(1)}, bf16[4,32,1024]{2,1,0:T(8,128)(2,1)}, u32[]{:S(2)}, u32[]{:S(2)}) %collective-permute-start.3) | collective-permute-done | bytes 262176 | tf_op jit(solution)/shard_map/ppermute | solution.py:11
  53.4 2.4 %multiply_convert_fusion = bf16[896,1024]{1,0:T(8,128)(2,1)} fusion(bf16[512,896]{1,0:T(8,128)(2,1)S(1)} %bitcast.73, bf16[512,1024]{1,0:T(8,128)(2,1)S(1)} %bitcast.69), kind=kOutput, calls=%fused_computation | convolution fusion | flops 941359104 | bytes 3801088 | tf_op jit(solution)/shard_map/dot_general | solution.py:111
  55.8 6.7 %collective-permute-done.2 = bf16[8,32,1024]{2,1,0:T(8,128)(2,1)S(1)} collective-permute-done((bf16[8,32,1024]{2,1,0:T(8,128)(2,1)S(1)}, bf16[8,32,1024]{2,1,0:T(8,128)(2,1)S(1)}, u32[]{:S(2)}, u32[]{:S(2)}) %collective-permute-start.2) | collective-permute-done | bytes 524320 | tf_op jit(solution)/shard_map/ppermute | solution.py:50
  63.5 6.6 %all-to-all-start = ((bf16[8,32,1024]{2,1,0:T(8,128)(2,1)}), bf16[8,32,1024]{2,1,0:T(8,128)(2,1)S(1)}, u32[]{:S(2)}, u32[]{:S(2)}) async-start(bf16[8,32,1024]{2,1,0:T(8,128)(2,1)} %add_convert_fusion), calls=%async_computation | async-start | bytes 1048576 | tf_op jit(solution)/shard_map/all_to_all | solution.py:56
  70.1 2.7 %dynamic-slice_bitcast_fusion.2 = (bf16[2,112,1024]{2,1,0:T(8,128)(2,1)}, bf16[2,112,1024]{2,1,0:T(8,128)(2,1)}, bf16[2,112,1024]{2,1,0:T(8,128)(2,1)}, bf16[2,112,1024]{2,1,0:T(8,128)(2,1)S(1)}) fusion(bf16[4,2,112,1024]{3,2,1,0:T(8,128)(2,1)} %bitcast.64, s32[]{:T(128)S(6)} %select_n.230, s32[]{:T(128)S(6)} %select_n.229, s32[]{:T(128)S(6)} %select_n.228, ...), kind=kLoop, calls=%fused_computation.27 | loop fusion | bytes 3670032 | tf_op jit(solution)/shard_map/jit(dynamic_index_in_dim)/squeeze | solution.py:15
  72.8 4.9 %collective-permute-start.10 = (bf16[2,112,1024]{2,1,0:T(8,128)(2,1)}, bf16[2,112,1024]{2,1,0:T(8,128)(2,1)}, u32[]{:S(2)}, u32[]{:S(2)}) collective-permute-start(bf16[2,112,1024]{2,1,0:T(8,128)(2,1)} %get-tuple-element.33), channel_id=1, source_target_pairs={{0,384},{64,448},{128,0},{192,64},{256,128},{320,192},{384,256},{4... | collective-permute-start | bytes 1376264 | tf_op jit(solution)/shard_map/ppermute | solution.py:67
  77.7 1.9 %collective-permute-start.9 = (bf16[2,112,1024]{2,1,0:T(8,128)(2,1)}, bf16[2,112,1024]{2,1,0:T(8,128)(2,1)}, u32[]{:S(2)}, u32[]{:S(2)}) collective-permute-start(bf16[2,112,1024]{2,1,0:T(8,128)(2,1)} %get-tuple-element.32), channel_id=1, source_target_pairs={{0,128},{64,192},{128,256},{192,320},{256,384},{320,448},{384,0},{... | collective-permute-start | bytes 1376264 | tf_op jit(solution)/shard_map/ppermute | solution.py:67
  79.6 4.1 %collective-permute-start.8 = (bf16[2,112,1024]{2,1,0:T(8,128)(2,1)}, bf16[2,112,1024]{2,1,0:T(8,128)(2,1)}, u32[]{:S(2)}, u32[]{:S(2)}) collective-permute-start(bf16[2,112,1024]{2,1,0:T(8,128)(2,1)} %get-tuple-element.31), channel_id=1, source_target_pairs={{0,256},{64,320},{128,384},{192,448},{256,0},{320,64},{384,128},{4... | collective-permute-start | bytes 1376264 | tf_op jit(solution)/shard_map/ppermute | solution.py:67
  83.7 1.3 %convolution_convert_fusion.1 = bf16[512,896]{1,0:T(8,128)(2,1)S(1)} fusion(bf16[512,1024]{1,0:T(8,128)(2,1)S(1)} %bitcast.70, bf16[896,1024]{1,0:T(8,128)(2,1)S(1)} %copy-done), kind=kOutput, calls=%fused_computation.2 | convolution fusion | flops 939982848 | bytes 3801088 | tf_op jit(solution)/shard_map/dot_general | solution.py:118
  85.9 1.9 %collective-permute-start.6 = (bf16[2,128,896]{2,1,0:T(8,128)(2,1)}, bf16[2,128,896]{2,1,0:T(8,128)(2,1)}, u32[]{:S(2)}, u32[]{:S(2)}) collective-permute-start(bf16[2,128,896]{2,1,0:T(8,128)(2,1)} %get-tuple-element.28), channel_id=1, source_target_pairs={{0,1},{1,0},{2,3},{3,2},{4,5},{5,4},{6,7},{7,6},{8,9},{9,8},{10,11... | collective-permute-start | bytes 1376264 | tf_op jit(solution)/shard_map/ppermute | solution.py:81
  87.8 9.1 %collective-permute-done.10 = bf16[2,112,1024]{2,1,0:T(8,128)(2,1)} collective-permute-done((bf16[2,112,1024]{2,1,0:T(8,128)(2,1)}, bf16[2,112,1024]{2,1,0:T(8,128)(2,1)}, u32[]{:S(2)}, u32[]{:S(2)}) %collective-permute-start.10) | collective-permute-done | bytes 458784 | tf_op jit(solution)/shard_map/ppermute | solution.py:67
  96.9 5.3 %collective-permute-done.9 = bf16[2,112,1024]{2,1,0:T(8,128)(2,1)} collective-permute-done((bf16[2,112,1024]{2,1,0:T(8,128)(2,1)}, bf16[2,112,1024]{2,1,0:T(8,128)(2,1)}, u32[]{:S(2)}, u32[]{:S(2)}) %collective-permute-start.9) | collective-permute-done | bytes 458784 | tf_op jit(solution)/shard_map/ppermute | solution.py:67
  102.2 1.6 %convert_add_fusion = f32[2,112,1024]{2,1,0:T(8,128)S(1)} fusion(bf16[2,112,1024]{2,1,0:T(8,128)(2,1)} %collective-permute-done.10, bf16[2,112,1024]{2,1,0:T(8,128)(2,1)} %collective-permute-done.9, bf16[2,112,1024]{2,1,0:T(8,128)(2,1)} %collective-permute-done.8, bf16[2,112,1024]{2,1,0:T(8,128)(2,1)S(1)} %get-tuple-element.30), kind=kLoop, calls=%fused_computation.6 | loop fusion | flops 1605632 | bytes 2752512 | tf_op jit(solution)/shard_map/add | solution.py:68
  103.9 4.8 %collective-permute-start.11 = (bf16[112,1024]{1,0:T(8,128)(2,1)S(1)}, bf16[112,1024]{1,0:T(8,128)(2,1)S(1)}, u32[]{:S(2)}, u32[]{:S(2)}) collective-permute-start(bf16[112,1024]{1,0:T(8,128)(2,1)S(1)} %fusion.9), channel_id=1, source_target_pairs={{0,64},{64,0},{128,192},{192,128},{256,320},{320,256},{384,448},{4... | collective-permute-start | bytes 688136 | tf_op jit(solution)/shard_map/ppermute | solution.py:70
  109.8 2.1 %collective-permute-start.7 = (bf16[128,896]{1,0:T(8,128)(2,1)S(1)}, bf16[128,896]{1,0:T(8,128)(2,1)S(1)}, u32[]{:S(2)}, u32[]{:S(2)}) collective-permute-start(bf16[128,896]{1,0:T(8,128)(2,1)S(1)} %fusion.8), channel_id=1, source_target_pairs={{0,2},{1,3},{2,0},{3,1},{4,6},{5,7},{6,4},{7,5},{8,10},{9,11},{10,... | collective-permute-start | bytes 688136 | tf_op jit(solution)/shard_map/ppermute | solution.py:84
  112.0 3.9 %collective-permute-done.11 = bf16[112,1024]{1,0:T(8,128)(2,1)S(1)} collective-permute-done((bf16[112,1024]{1,0:T(8,128)(2,1)S(1)}, bf16[112,1024]{1,0:T(8,128)(2,1)S(1)}, u32[]{:S(2)}, u32[]{:S(2)}) %collective-permute-start.11) | collective-permute-done | bytes 229408 | tf_op jit(solution)/shard_map/ppermute | solution.py:70
  (38 shorter events, 10.7 us)
Async XLA Ops:
  0.6 43.1 %copy-start = (bf16[896,1024]{1,0:T(8,128)(2,1)S(1)}, bf16[896,1024]{1,0:T(8,128)(2,1)}, u32[]{:S(2)}) copy-start(bf16[896,1024]{1,0:T(8,128)(2,1)} %param.7) | copy-start | bytes 5505028
  2.0 29.3 %collective-permute-start = (bf16[128,896]{1,0:T(8,128)(2,1)S(1)}, bf16[128,896]{1,0:T(8,128)(2,1)S(1)}, u32[]{:S(2)}, u32[]{:S(2)}) collective-permute-start(bf16[128,896]{1,0:T(8,128)(2,1)S(1)} %fusion), channel_id=1, source_target_pairs={{0,2},{1,3},{2,0},{3,1},{4,6},{5,7},{6,4},{7,5},{8,10},{9,11},{10,... | collective-permute-start | bytes 688136 | tf_op jit(solution)/shard_map/ppermute | solution.py:95
  31.4 11.1 %collective-permute-start.1 = (bf16[2,128,896]{2,1,0:T(8,128)(2,1)S(1)}, bf16[2,128,896]{2,1,0:T(8,128)(2,1)S(1)}, u32[]{:S(2)}, u32[]{:S(2)}) collective-permute-start(bf16[2,128,896]{2,1,0:T(8,128)(2,1)S(1)} %pad_maximum_fusion.2), channel_id=1, source_target_pairs={{0,1},{1,0},{2,3},{3,2},{4,5},{5,4},{6,7},{7,6},{8,9},{9,8},{10,11... | collective-permute-start | bytes 1376264 | tf_op jit(solution)/shard_map/ppermute | solution.py:100
  33.3 15.1 %collective-permute-start.4 = (bf16[4,32,1024]{2,1,0:T(8,128)(2,1)S(1)}, bf16[4,32,1024]{2,1,0:T(8,128)(2,1)}, u32[]{:S(2)}, u32[]{:S(2)}) collective-permute-start(bf16[4,32,1024]{2,1,0:T(8,128)(2,1)S(1)} %bitcast.65), channel_id=1, source_target_pairs={{0,8},{1,57},{2,10},{3,59},{4,12},{5,61},{6,14},{7,63},{8,16},{9,1... | collective-permute-start | bytes 786440 | tf_op jit(solution)/shard_map/ppermute | solution.py:28
  36.6 11.8 %collective-permute-start.5 = (bf16[4,32,1024]{2,1,0:T(8,128)(2,1)S(1)}, bf16[4,32,1024]{2,1,0:T(8,128)(2,1)}, u32[]{:S(2)}, u32[]{:S(2)}) collective-permute-start(bf16[4,32,1024]{2,1,0:T(8,128)(2,1)S(1)} %bitcast.66), channel_id=1, source_target_pairs={{0,60},{4,0},{8,4},{12,8},{16,12},{20,16},{24,20},{28,24},{32,28},... | collective-permute-start | bytes 786440 | tf_op jit(solution)/shard_map/ppermute | solution.py:11
  39.7 12.3 %collective-permute-start.3 = (bf16[4,32,1024]{2,1,0:T(8,128)(2,1)S(1)}, bf16[4,32,1024]{2,1,0:T(8,128)(2,1)}, u32[]{:S(2)}, u32[]{:S(2)}) collective-permute-start(bf16[4,32,1024]{2,1,0:T(8,128)(2,1)S(1)} %bitcast.67), channel_id=1, source_target_pairs={{0,4},{4,8},{8,12},{12,16},{16,20},{20,24},{24,28},{28,32},{32,36}... | collective-permute-start | bytes 786440 | tf_op jit(solution)/shard_map/ppermute | solution.py:11
  42.8 0.9 copy-start.3
  45.1 8.2 %copy-start.4 = (bf16[2,2,128,896]{3,2,1,0:T(8,128)(2,1)S(1)}, bf16[2,2,128,896]{3,2,1,0:T(8,128)(2,1)}, u32[]{:S(2)}) copy-start(bf16[2,2,128,896]{3,2,1,0:T(8,128)(2,1)} %copy-done.3) | copy-start | bytes 2752516
  45.1 17.3 %collective-permute-start.2 = (bf16[8,32,1024]{2,1,0:T(8,128)(2,1)S(1)}, bf16[8,32,1024]{2,1,0:T(8,128)(2,1)S(1)}, u32[]{:S(2)}, u32[]{:S(2)}) collective-permute-start(bf16[8,32,1024]{2,1,0:T(8,128)(2,1)S(1)} %get-tuple-element.22), channel_id=1, source_target_pairs={{0,4},{4,0},{8,12},{12,8},{16,20},{20,16},{24,28},{28,24},{32,36},... | collective-permute-start | bytes 1572872 | tf_op jit(solution)/shard_map/ppermute | solution.py:50
  53.3 2.4 %copy-start.1 = (bf16[4,4,32,1024]{3,2,1,0:T(8,128)(2,1)}, bf16[4,4,32,1024]{3,2,1,0:T(8,128)(2,1)S(1)}, u32[]{:S(2)}) copy-start(bf16[4,4,32,1024]{3,2,1,0:T(8,128)(2,1)S(1)} %pad_maximum_fusion) | copy-start | bytes 3145732
  63.5 55.4 %all-to-all-start = ((bf16[8,32,1024]{2,1,0:T(8,128)(2,1)}), bf16[8,32,1024]{2,1,0:T(8,128)(2,1)S(1)}, u32[]{:S(2)}, u32[]{:S(2)}) async-start(bf16[8,32,1024]{2,1,0:T(8,128)(2,1)} %add_convert_fusion), calls=%async_computation | async-start | bytes 1048576 | tf_op jit(solution)/shard_map/all_to_all | solution.py:56
  70.1 13.6 %copy-start.2 = (bf16[4,4,32,1024]{3,2,1,0:T(8,128)(2,1)S(1)}, bf16[4,4,32,1024]{3,2,1,0:T(8,128)(2,1)}, u32[]{:S(2)}) copy-start(bf16[4,4,32,1024]{3,2,1,0:T(8,128)(2,1)} %copy-done.1) | copy-start | bytes 3145732
  72.8 24.1 %collective-permute-start.10 = (bf16[2,112,1024]{2,1,0:T(8,128)(2,1)}, bf16[2,112,1024]{2,1,0:T(8,128)(2,1)}, u32[]{:S(2)}, u32[]{:S(2)}) collective-permute-start(bf16[2,112,1024]{2,1,0:T(8,128)(2,1)} %get-tuple-element.33), channel_id=1, source_target_pairs={{0,384},{64,448},{128,0},{192,64},{256,128},{320,192},{384,256},{4... | collective-permute-start | bytes 1376264 | tf_op jit(solution)/shard_map/ppermute | solution.py:67
  77.7 24.6 %collective-permute-start.9 = (bf16[2,112,1024]{2,1,0:T(8,128)(2,1)}, bf16[2,112,1024]{2,1,0:T(8,128)(2,1)}, u32[]{:S(2)}, u32[]{:S(2)}) collective-permute-start(bf16[2,112,1024]{2,1,0:T(8,128)(2,1)} %get-tuple-element.32), channel_id=1, source_target_pairs={{0,128},{64,192},{128,256},{192,320},{256,384},{320,448},{384,0},{... | collective-permute-start | bytes 1376264 | tf_op jit(solution)/shard_map/ppermute | solution.py:67
  79.6 22.6 %collective-permute-start.8 = (bf16[2,112,1024]{2,1,0:T(8,128)(2,1)}, bf16[2,112,1024]{2,1,0:T(8,128)(2,1)}, u32[]{:S(2)}, u32[]{:S(2)}) collective-permute-start(bf16[2,112,1024]{2,1,0:T(8,128)(2,1)} %get-tuple-element.31), channel_id=1, source_target_pairs={{0,256},{64,320},{128,384},{192,448},{256,0},{320,64},{384,128},{4... | collective-permute-start | bytes 1376264 | tf_op jit(solution)/shard_map/ppermute | solution.py:67
  85.9 22.8 %collective-permute-start.6 = (bf16[2,128,896]{2,1,0:T(8,128)(2,1)}, bf16[2,128,896]{2,1,0:T(8,128)(2,1)}, u32[]{:S(2)}, u32[]{:S(2)}) collective-permute-start(bf16[2,128,896]{2,1,0:T(8,128)(2,1)} %get-tuple-element.28), channel_id=1, source_target_pairs={{0,1},{1,0},{2,3},{3,2},{4,5},{5,4},{6,7},{7,6},{8,9},{9,8},{10,11... | collective-permute-start | bytes 1376264 | tf_op jit(solution)/shard_map/ppermute | solution.py:81
  103.9 13.9 %copy-start.5 = (bf16[128,896]{1,0:T(8,128)(2,1)S(1)}, bf16[128,896]{1,0:T(8,128)(2,1)}, u32[]{:S(2)}) copy-start(bf16[128,896]{1,0:T(8,128)(2,1)} %param.5) | copy-start | bytes 688132
  103.9 13.9 %copy-start.6 = (bf16[128,896]{1,0:T(8,128)(2,1)S(1)}, bf16[128,896]{1,0:T(8,128)(2,1)}, u32[]{:S(2)}) copy-start(bf16[128,896]{1,0:T(8,128)(2,1)} %param.4) | copy-start | bytes 688132
  103.9 12.0 %collective-permute-start.11 = (bf16[112,1024]{1,0:T(8,128)(2,1)S(1)}, bf16[112,1024]{1,0:T(8,128)(2,1)S(1)}, u32[]{:S(2)}, u32[]{:S(2)}) collective-permute-start(bf16[112,1024]{1,0:T(8,128)(2,1)S(1)} %fusion.9), channel_id=1, source_target_pairs={{0,64},{64,0},{128,192},{192,128},{256,320},{320,256},{384,448},{4... | collective-permute-start | bytes 688136 | tf_op jit(solution)/shard_map/ppermute | solution.py:70
  109.8 7.9 %collective-permute-start.7 = (bf16[128,896]{1,0:T(8,128)(2,1)S(1)}, bf16[128,896]{1,0:T(8,128)(2,1)S(1)}, u32[]{:S(2)}, u32[]{:S(2)}) collective-permute-start(bf16[128,896]{1,0:T(8,128)(2,1)S(1)} %fusion.8), channel_id=1, source_target_pairs={{0,2},{1,3},{2,0},{3,1},{4,6},{5,7},{6,4},{7,5},{8,10},{9,11},{10,... | collective-permute-start | bytes 688136 | tf_op jit(solution)/shard_map/ppermute | solution.py:84
